TPU v7x, 32 devices: a whole 2x2x4 slice. The times are simulated.
32 devices in a mesh: dp: 4 (over y, x), expert: 8 (over z, core).
Axes of the slice: x: 2, y: 2, z: 4, core: 2. Of those that a mesh axis runs over, the one named last changes fastest.
Arguments:
- tokens: bfloat16 [4096, 1536], P('expert'), may hold values from -6 to 6
- past_len: int32 [32], P('expert'), may hold values from 1 to 4608
- cache_keys: bfloat16 [32, 4608, 512], P('expert', None, 'dp'), may hold values from -32 to 32
- cache_values: bfloat16 [32, 4608, 512], P('expert', None, 'dp'), may hold values from -6 to 6
- attn_gain: float32 [1536], replicated, may hold values from 0.1 to 1.9
- w_query: bfloat16 [1536, 1536], P(None, 'dp'), may hold values from -3 to 3
- w_key: bfloat16 [1536, 512], P(None, 'dp'), may hold values from -0.15625 to 0.15625
- w_value: bfloat16 [1536, 512], P(None, 'dp'), may hold values from -0.15625 to 0.15625
- w_out: bfloat16 [1536, 1536], P('dp'), may hold values from -0.15625 to 0.15625
- moe_gain: float32 [1536], replicated, may hold values from 0.1 to 1.9
- router: bfloat16 [1536, 40], replicated, may hold values from -16 to 16
- expert_in: bfloat16 [64, 1536, 1024], P('expert'), may hold values from -0.15625 to 0.15625
- expert_out: bfloat16 [64, 512, 1536], P('expert'), may hold values from -1 to 1
- final_gain: float32 [1536], replicated, may hold values from 0.1 to 1.9
- slot_owner: int32 [64], replicated, may hold values from 0 to 39, as said below
- routes: int32 [4096, 8], P(('expert', 'dp')), may hold values from 0 to 39, all different within a row; in each aligned block of 128 rows (0 to 127, 128 to 255, ...) at most 40 rows name the same one
- split_pick: int32 [4096, 8], P(('expert', 'dp')), may hold values from 0 to 2519
Outputs:
- output: bfloat16 [4096, 1536], P(('expert', 'dp'))
Inputs may be any that keep to these rules, and one draw needn't show every extreme that they name: `routes`: each row names 8 different experts; at most 40 rows of one device name one expert, a bound that some block reaches. `slot_owner`: every expert is served by at least one slot.
All inputs are finite; a program needn't handle non-finite values.
Results may differ from a plain program's by a relative error of at most 0.025.
Values may be sent and summed in bfloat16 or wider, within the bound.
A program may use at most 128 MiB of HBM per device.

v0:
```python
import math

import jax
import jax.numpy as jnp
from jax import lax
from jax.sharding import PartitionSpec as P

HD = 64
SINK = 4
WINDOW = 4096


epsilon = 1e-05
neg_large = -1e30


def rms_scale(values, gain):
    widened = values.astype(jnp.float32)
    mean_square = jnp.mean(widened * widened, axis=-1, keepdims=True)
    return widened * lax.rsqrt(mean_square + epsilon) * gain


def block_update(carried, scores, live, values_part):
    top_old, total_old, accum_old = carried
    masked = jnp.where(live, scores, neg_large)
    top_new = jnp.maximum(top_old, jnp.max(masked, axis=-1))
    weights = jnp.where(live, jnp.exp(masked - top_new[..., None]), 0.0)
    factor = jnp.exp(top_old - top_new)
    total_new = total_old * factor + jnp.sum(weights, axis=-1)
    contrib = jnp.einsum(
        "rkmp,rpkd->rkmd",
        weights.astype(jnp.bfloat16),
        values_part,
        preferred_element_type=jnp.float32,
    )
    return (top_new, total_new, accum_old * factor[..., None] + contrib)


def past_block(carried, start_slot, queries, keys_all, values_all, lengths, key_block, per_request):
    count, kv_local, row_total, head_dim = queries.shape
    keys_part = lax.dynamic_slice_in_dim(keys_all, start_slot, key_block, 1).reshape(
        count, key_block, kv_local, head_dim
    )
    values_part = lax.dynamic_slice_in_dim(values_all, start_slot, key_block, 1).reshape(
        count, key_block, kv_local, head_dim
    )
    scores = jnp.einsum(
        "rkmd,rpkd->rkmp", queries, keys_part, preferred_element_type=jnp.float32
    ) * head_dim ** (-0.5)
    place = start_slot + jnp.arange(key_block, dtype=jnp.int32)
    query_pos = jnp.arange(row_total, dtype=jnp.int32) % per_request
    bound = lengths[:, None, None]
    live = (place[None, None, :] < bound) & (
        (place[None, None, :] < SINK)
        | (place[None, None, :] >= bound + query_pos[None, :, None] - WINDOW + 1)
    )
    return block_update(carried, scores, live[:, None], values_part)


def shards(
    tokens,
    past_len,
    cache_keys,
    cache_values,
    attn_gain,
    w_query,
    w_key,
    w_value,
    w_out,
    moe_gain,
    router,
    expert_in,
    expert_out,
    final_gain,
    slot_owner,
    routes,
    split_pick,
):
    requests = past_len.shape[0]
    group_rows = tokens.shape[0]
    width = tokens.shape[1]
    per_request = group_rows // requests
    head_dim = HD
    kv_local = w_key.shape[1] // head_dim
    query_heads = w_query.shape[1] // head_dim
    share_count = query_heads // kv_local
    capacity = cache_keys.shape[1]
    key_block = math.gcd(capacity, 512)
    row_total = share_count * per_request
    normed = rms_scale(tokens, attn_gain).astype(jnp.bfloat16)
    queries = jnp.dot(normed, w_query, preferred_element_type=jnp.float32).astype(jnp.bfloat16)
    keys_new = jnp.dot(normed, w_key, preferred_element_type=jnp.float32).astype(jnp.bfloat16)
    values_new = jnp.dot(normed, w_value, preferred_element_type=jnp.float32).astype(jnp.bfloat16)
    query_grid = (
        queries.reshape(requests, per_request, kv_local, share_count, head_dim)
        .transpose(0, 2, 3, 1, 4)
        .reshape(requests, kv_local, row_total, head_dim)
    )
    keys_new = keys_new.reshape(requests, per_request, kv_local, head_dim)
    values_new = values_new.reshape(requests, per_request, kv_local, head_dim)
    start_state = (
        jnp.full((requests, kv_local, row_total), neg_large, jnp.float32),
        jnp.zeros((requests, kv_local, row_total), jnp.float32),
        jnp.zeros((requests, kv_local, row_total, head_dim), jnp.float32),
    )

    def visit_block(block_idx, carried):
        return past_block(
            carried,
            block_idx * key_block,
            query_grid,
            cache_keys,
            cache_values,
            past_len,
            key_block,
            per_request,
        )

    carried = lax.fori_loop(0, capacity // key_block, visit_block, start_state)
    new_scores = jnp.einsum(
        "rkmd,rpkd->rkmp", query_grid, keys_new, preferred_element_type=jnp.float32
    ) * head_dim ** (-0.5)
    query_pos = jnp.arange(row_total, dtype=jnp.int32) % per_request
    live_new = jnp.arange(per_request, dtype=jnp.int32)[None, :] <= query_pos[:, None]
    top_final, total_final, accum_final = block_update(
        carried, new_scores, live_new[None, None], values_new
    )
    heads = accum_final / total_final[..., None]
    heads = (
        heads.reshape(requests, kv_local, share_count, per_request, head_dim)
        .transpose(0, 3, 1, 2, 4)
        .reshape(group_rows, query_heads * head_dim)
        .astype(jnp.bfloat16)
    )
    tok_dev = group_rows // lax.axis_size("dp")
    attn_rows = lax.psum_scatter(
        jnp.dot(heads, w_out, preferred_element_type=jnp.float32).astype(jnp.bfloat16),
        "dp",
        scatter_dimension=0,
        tiled=True,
    ).astype(jnp.float32)
    rows_mine = lax.dynamic_slice_in_dim(tokens, lax.axis_index("dp") * tok_dev, tok_dev, 0)
    stream = rows_mine.astype(jnp.float32) + attn_rows
    moe_in = rms_scale(stream, moe_gain).astype(jnp.bfloat16)
    logits = jnp.dot(moe_in, router, preferred_element_type=jnp.float32)
    expert_ids = jnp.arange(router.shape[1], dtype=jnp.int32)
    picked = routes[:, :, None] == expert_ids[None, None, :]
    chosen = jnp.sum(jnp.where(picked, logits[:, None, :], 0.0), axis=-1)
    gates = jax.nn.softmax(chosen, axis=-1)
    slot_total = slot_owner.shape[0]
    slot_local = expert_in.shape[0]
    top_count = routes.shape[1]
    most_rows = max(2, tok_dev * top_count * 5 // (2 * slot_total))
    slot_ids = jnp.arange(slot_total, dtype=jnp.int32)
    same_owner = slot_owner[:, None] == slot_owner[None, :]
    slot_rank = jnp.sum(
        (same_owner & (slot_ids[None, :] < slot_ids[:, None])).astype(jnp.int32), axis=1
    )
    serving = slot_owner[None, None, :] == routes[:, :, None]
    replicas = jnp.sum(serving.astype(jnp.int32), axis=-1)
    wanted = split_pick % replicas
    target = jnp.sum(
        jnp.where(
            serving & (slot_rank[None, None, :] == wanted[:, :, None]), slot_ids[None, None, :], 0
        ),
        axis=-1,
    )
    route_count = tok_dev * top_count
    flat_slot = target.reshape(route_count)
    one_hot = (flat_slot[:, None] == slot_ids[None, :]).astype(jnp.int32)
    earlier = jnp.cumsum(one_hot, axis=0) - one_hot
    within = jnp.sum(earlier * one_hot, axis=1)
    location = flat_slot * most_rows + within
    source_index = jnp.arange(route_count, dtype=jnp.int32) // top_count
    outgoing = (
        jnp.zeros((slot_total * most_rows, width), jnp.bfloat16)
        .at[location]
        .set(moe_in[source_index])
    )
    outgoing = outgoing.reshape(lax.axis_size("expert"), slot_local, most_rows, width)
    ff_width = expert_out.shape[1]
    gate_up = jnp.einsum(
        "nsmd,sdf->snmf",
        lax.all_to_all(outgoing, "expert", split_axis=0, concat_axis=0, tiled=True),
        expert_in,
        preferred_element_type=jnp.float32,
    )
    activation = (jax.nn.silu(gate_up[..., :ff_width]) * gate_up[..., ff_width:]).astype(
        jnp.bfloat16
    )
    produced = jnp.einsum(
        "snmf,sfd->nsmd", activation, expert_out, preferred_element_type=jnp.float32
    ).astype(jnp.bfloat16)
    returned = lax.all_to_all(produced, "expert", split_axis=0, concat_axis=0, tiled=True)
    expert_rows = returned.reshape(slot_total * most_rows, width)[location].reshape(
        tok_dev, top_count, width
    )
    combined = stream + jnp.sum(gates[:, :, None] * expert_rows.astype(jnp.float32), axis=1)
    return rms_scale(combined, final_gain).astype(jnp.bfloat16)


def solution(mesh):
    return jax.shard_map(
        shards,
        mesh=mesh,
        in_specs=(
            P("expert", None),
            P("expert"),
            P("expert", None, "dp"),
            P("expert", None, "dp"),
            P(),
            P(None, "dp"),
            P(None, "dp"),
            P(None, "dp"),
            P("dp", None),
            P(),
            P(),
            P("expert", None, None),
            P("expert", None, None),
            P(),
            P(),
            P(("expert", "dp"), None),
            P(("expert", "dp"), None),
        ),
        out_specs=P(("expert", "dp"), None),
        check_vma=False,
    )
```

profile of v0, /device:TPU:0, one launch (start us, length us, event | category | flops | bytes accessed | tf_op | source)
XLA Modules:
  0.0 594.1 jit_solution(2102625653123660433)
XLA Ops:
  6.6 1.9 fusion.28
  9.2 2.1 convolution_convert_fusion.3
  12.2 1.6 convolution_convert_fusion.2
  14.7 2.3 convolution_convert_fusion.1
  18.7 96.0 %while.22 = (s32[]{:T(128)}, f32[4,2,384]{2,1,0:T(2,128)S(1)}, f32[4,2,384]{2,1,0:T(2,128)}, f32[4,2,384,64]{2,3,1,0:T(8,128)}, s32[4]{0:T(128)S(1)}, /*index=5*...) while((s32[]{:T(128)}, f32[4,2,384]{2,1,0:T(2,128)S(1)}, ...), condition=%wide.region_4.5_spmd.clone, body=%wide.region_1.4_spmd.clone.sunk | while | flops 426073856 | bytes 35842384 | solution.py:119
  19.4 1.4 or_and_fusion.2
  20.8 1.3 constant_dynamic-slice_fusion.3
  22.5 2.4 fusion.88
  24.9 1.7 fusion.90
  26.7 2.3 fusion.92
  30.0 1.4 or_and_fusion.2
  31.4 1.3 constant_dynamic-slice_fusion.3
  33.1 2.4 fusion.88
  35.5 1.7 fusion.90
  37.3 2.3 fusion.92
  40.6 1.4 or_and_fusion.2
  42.0 1.3 constant_dynamic-slice_fusion.3
  43.7 2.4 fusion.88
  46.1 1.7 fusion.90
  47.9 2.3 fusion.92
  51.2 1.4 or_and_fusion.2
  52.6 1.3 constant_dynamic-slice_fusion.3
  54.3 2.4 fusion.88
  56.8 1.7 fusion.90
  58.5 2.3 fusion.92
  61.8 1.4 or_and_fusion.2
  63.2 1.3 constant_dynamic-slice_fusion.3
  65.0 2.4 fusion.88
  67.4 1.7 fusion.90
  69.1 2.3 fusion.92
  72.4 1.4 or_and_fusion.2
  73.8 1.3 constant_dynamic-slice_fusion.3
  75.6 2.4 fusion.88
  78.0 1.7 fusion.90
  79.7 2.3 fusion.92
  83.0 1.4 or_and_fusion.2
  84.4 1.3 constant_dynamic-slice_fusion.3
  86.2 2.4 fusion.88
  88.6 1.7 fusion.90
  90.3 2.3 fusion.92
  93.7 1.4 or_and_fusion.2
  95.1 1.3 constant_dynamic-slice_fusion.3
  96.8 2.4 fusion.88
  99.2 1.7 fusion.90
  100.9 2.3 fusion.92
  104.3 1.4 or_and_fusion.2
  105.7 1.3 constant_dynamic-slice_fusion.3
  107.4 2.4 fusion.88
  109.8 1.7 fusion.90
  111.6 2.3 fusion.92
  114.7 1.5 fusion.63
  118.4 2.2 convolution_convert_fusion
  121.7 18.0 %reduce-window.6 = s32[64,8,128]{2,1,0:T(8,128)S(1)} reduce-window(s32[64,8,128]{2,1,0:T(8,128)S(1)} %fusion.51, s32[]{:T(128)} %constant.212.clone.1), window={size=1x1x128 pad=0_0x0_0x127_0}, to_apply=%region_15.16 | reduce-window | flops 8323072 | bytes 524292 | tf_op jit(solution)/shard_map/reduce-window
  140.4 14.2 %reduce-scatter.2.cloned.1.call-done = bf16[128,1536]{1,0:T(8,128)(2,1)} async-done(((bf16[512,1536]{1,0:T(8,128)(2,1)}), bf16[128,1536]{1,0:T(8,128)(2,1)}) %reduce-scatter.2.cloned.1.call-update) | async-done | bytes 393232 | tf_op jit(solution)/shard_map/reduce_scatter | solution.py:136
  154.6 1.2 multiply_reduce_fusion.1
  157.0 20.7 %scatter_custom_fusion = bf16[2560,1536]{1,0:T(8,128)(2,1)} fusion(s32[1024]{0:T(1024)S(1)} %bitcast.118, bf16[]{:T(256)} %constant.221.clone.1, bf16[128,1536]{1,0:T(8,128)(2,1)S(1)} %multiply_convert_fusion.1, s32[1024]{0:T(1024)S(1)} %broadcast_clamp_fusion.1), kind=kCustom, calls=%fused_computation.42 | custom fusion | bytes 7864322 | tf_op jit(solution)/shard_map/scatter | solution.py:178
  177.7 178.7 %all_to_all.10 = bf16[8,8,40,1536]{3,2,1,0:T(8,128)(2,1)} all-to-all(bf16[8,8,40,1536]{3,2,1,0:T(8,128)(2,1)} %bitcast.105), channel_id=1, replica_groups=mesh['dp'=4,'expert'=8] {'expert'}, dimensions={0} | all-to-all | bytes 15728640 | tf_op jit(solution)/shard_map/all_to_all | solution.py:184
  356.4 20.2 %fusion.17 = f32[8,8,40,1024]{3,2,1,0:T(8,128)} fusion(bf16[8,1536,1024]{2,1,0:T(8,128)(2,1)} %param.30, bf16[8,8,40,1536]{3,2,1,0:T(8,128)(2,1)} %all_to_all.10), kind=kOutput, calls=%fused_computation.32 | convolution fusion | flops 8053063680 | bytes 43515904 | tf_op jit(solution)/shard_map/nsmd,sdf->snmf/dot_general | solution.py:182
  376.6 10.8 %convert_bitcast_fusion = bf16[8,8,40,1536]{3,2,0,1:T(8,128)(2,1)S(1)} fusion(bf16[8,512,1536]{2,1,0:T(8,128)(2,1)} %param.31, f32[8,8,40,1024]{3,2,1,0:T(8,128)} %fusion.17), kind=kOutput, calls=%fused_computation.37 | convolution fusion | flops 4038328320 | bytes 30932992 | tf_op jit(solution)/shard_map/snmf,sfd->nsmd/dot_general | solution.py:191
  387.4 3.8 copy.85
  391.3 5.3 all-to-all-start.1
  397.0 172.2 %all-to-all-done.1 = bf16[8,8,40,1536]{3,2,1,0:T(8,128)(2,1)} async-done(((bf16[8,8,40,1536]{3,2,1,0:T(8,128)(2,1)}), bf16[8,8,40,1536]{3,2,1,0:T(8,128)(2,1)}, u32[]{:S(2)}, u32[]{:S(2)}) %all-to-all-start.1) | async-done | bytes 7864352 | tf_op jit(solution)/shard_map/all_to_all | solution.py:194
  569.2 11.7 %gather_fusion = bf16[1024,1536]{1,0:T(8,128)(2,1)} fusion(bf16[2560,1536]{1,0:T(8,128)(2,1)} %bitcast.13, s32[1024]{0:T(1024)S(1)} %broadcast_clamp_fusion), kind=kCustom, calls=%fused_computation.1 | custom fusion | bytes 6295552 | tf_op jit(solution)/shard_map/gather | solution.py:195
  580.9 4.8 fusion.22
  (251 shorter events, 24.2 us)
Async XLA Ops:
  6.5 111.9 %copy-start = (bf16[384,1536]{1,0:T(8,128)(2,1)S(1)}, bf16[384,1536]{1,0:T(8,128)(2,1)}, u32[]{:S(2)}) copy-start(bf16[384,1536]{1,0:T(8,128)(2,1)} %param.27) | copy-start | bytes 3538948
  6.5 5.6 copy-start.2
  6.5 5.6 copy-start.18
  6.5 148.1 %reduce-scatter.2.cloned.1.call-start = ((), (), s32[]{:S(2)}) async-start(), calls=%async_computation.3 | async-start | bytes 1966080 | tf_op jit(solution)/shard_map/reduce_scatter | solution.py:136
  16.9 1.7 copy-start.12
  24.9 1.7 copy-start.7
  24.9 1.8 copy-start.19
  26.7 2.3 copy-start.8
  28.9 0.9 copy-start.20
  35.5 1.7 copy-start.7
  35.5 1.8 copy-start.19
  37.3 2.3 copy-start.8
  39.6 0.9 copy-start.20
  46.1 1.7 copy-start.7
  46.1 1.8 copy-start.19
  47.9 2.3 copy-start.8
  50.2 0.9 copy-start.20
  56.7 1.7 copy-start.7
  56.7 1.8 copy-start.19
  58.5 2.3 copy-start.8
  60.8 0.9 copy-start.20
  67.3 1.7 copy-start.7
  67.4 1.8 copy-start.19
  69.1 2.3 copy-start.8
  71.4 0.9 copy-start.20
  78.0 1.7 copy-start.7
  78.0 1.8 copy-start.19
  79.7 2.3 copy-start.8
  82.0 0.9 copy-start.20
  88.6 1.7 copy-start.7
  88.6 1.8 copy-start.19
  90.3 2.3 copy-start.8
  92.6 0.9 copy-start.20
  99.2 1.7 copy-start.7
  99.2 1.8 copy-start.19
  100.9 2.3 copy-start.8
  103.2 0.9 copy-start.20
  109.8 1.7 copy-start.7
  109.8 1.8 copy-start.19
  111.5 2.3 copy-start.8
  113.8 0.9 copy-start.20
  114.7 2.7 copy-start.9
  114.7 2.7 copy-start.6
  114.7 2.7 copy-start.10
  114.7 2.7 copy-start.21
  117.9 2.8 copy-start.17
  117.9 2.9 copy-start.13
  117.9 3.0 copy-start.16
  118.4 36.2 %copy-start.3 = (bf16[512,1536]{1,0:T(8,128)(2,1)S(1)}, bf16[512,1536]{1,0:T(8,128)(2,1)}, u32[]{:S(2)}) copy-start(bf16[512,1536]{1,0:T(8,128)(2,1)} %param.19) | copy-start | bytes 4718596
  120.6 35.3 %copy-start.14 = (f32[1536]{0:T(1024)S(1)}, f32[1536]{0:T(1024)}, u32[]{:S(2)}) copy-start(f32[1536]{0:T(1024)} %param.28) | copy-start | bytes 18436
  391.3 5.3 copy-start.11
  391.3 177.9 %all-to-all-start.1 = ((bf16[8,8,40,1536]{3,2,1,0:T(8,128)(2,1)}), bf16[8,8,40,1536]{3,2,1,0:T(8,128)(2,1)}, u32[]{:S(2)}, u32[]{:S(2)}) async-start(bf16[8,8,40,1536]{3,2,1,0:T(8,128)(2,1)} %copy.85), calls=%async_computation.2 | async-start | bytes 15728640 | tf_op jit(solution)/shard_map/all_to_all | solution.py:194
  569.2 17.8 %copy-start.1 = (bf16[384,1536]{1,0:T(8,128)(2,1)S(1)}, bf16[384,1536]{1,0:T(8,128)(2,1)}, u32[]{:S(2)}) copy-start(bf16[384,1536]{1,0:T(8,128)(2,1)} %param.27) | copy-start | bytes 3538948
  580.9 4.9 copy-start.4
  580.9 4.9 copy-start.5
  580.9 5.1 copy-start.15
Sparse Core Ops, SparseCore 0:
  120.7 33.8 reduce-scatter.1
where the time goes:
time: 598 us; the launch traced here: 594 us
  waiting for transfers between devices  186 us (31%)
  blocking collectives  179 us (30%)
  matrix products  83 us (14%)
  local copies, waits for them, and re-layouts  64.4 us (11%)
  other arithmetic  60.6 us (10%)
  between operations  14.1 us (2%)
    all_to_all x1, blocking collectives, shards(): lax.all_to_all(outgoing, 'expert', split_axis=0, concat_axis=0, tiled=True)  179 us
    all_to_all x1, waiting for transfers between devices, shards(): lax.all_to_all(produced, 'expert', split_axis=0, concat_axis=0, tiled=True)  172 us
    dot_general x9, matrix products, past_block(): jnp.einsum('rkmd,rpkd->rkmp', queries, keys_part, preferred_element_type=...  21.3 us
    dot_general x10, matrix products, block_update(): jnp.einsum('rkmp,rpkd->rkmd', weights.astype(jnp.bfloat16), values_part,...  20.7 us
    scatter x1, local copies, waits for them, and re-layouts, shards(): outgoing = jnp.zeros((slot_total * most_rows, width), jnp.bfloat16).at[lo...  20.7 us
    dot_general x1, matrix products, shards(): jnp.einsum('nsmd,sdf->snmf', lax.all_to_all(outgoing, 'expert', split_axi...  20.2 us
    another operation x3, other arithmetic  18.2 us
    reduce_sum x10, other arithmetic, block_update(): total_new = total_old * factor + jnp.sum(weights, axis=-1)  16.3 us
  transfers between devices with their start and end apart: 2, of which 2 were waited for; matrix products, arithmetic and copies ran while one was open for 3% of the time, Pallas kernels for 0%

commit v1 on v0

v1 whole, which is shorter than its diff:
```python
import functools
import math

import jax
import jax.numpy as jnp
from jax import lax
from jax.experimental import pallas as pl
from jax.experimental.pallas import tpu as pltpu
from jax.sharding import PartitionSpec as P

HD = 64
SINK = 4
WINDOW = 4096
MOST_ROWS = 2048

epsilon = 1e-05
neg_large = -1e30


def rms_scale(values, gain):
    widened = values.astype(jnp.float32)
    mean_square = jnp.mean(widened * widened, axis=-1, keepdims=True)
    return widened * lax.rsqrt(mean_square + epsilon) * gain


def mm(a, b):
    return jnp.dot(a, b, preferred_element_type=jnp.float32)


def attend_kernel(
    key_block, len_ref, tok_ref, gain_ref, wq_ref, wk_ref, wv_ref, wo_ref, kc_ref, vc_ref,
    out_ref, qt_ref, top_ref, total_ref, acc_ref,
):
    length = len_ref[pl.program_id(0)]
    rows = tok_ref.shape[0]
    heads = wq_ref.shape[1] // HD
    kv_local = wk_ref.shape[1] // HD
    share = heads // kv_local
    columns = heads * rows
    normed = rms_scale(tok_ref[...], gain_ref[...]).astype(jnp.bfloat16)
    queries = mm(normed, wq_ref[...]).astype(jnp.bfloat16).astype(jnp.float32) * HD ** (-0.5)
    queries_t = queries.T.astype(jnp.bfloat16)
    qt_ref[...] = jnp.zeros_like(qt_ref)
    for h in range(heads):
        kv = h // share
        qt_ref[kv * HD : (kv + 1) * HD, h * rows : (h + 1) * rows] = queries_t[h * HD : (h + 1) * HD, :]
    keys_new = mm(normed, wk_ref[...]).astype(jnp.bfloat16)
    values_new = mm(normed, wv_ref[...]).astype(jnp.bfloat16)

    def weigh(values, weights):
        return lax.dot_general(
            values, weights, (((0,), (0,)), ((), ())), preferred_element_type=jnp.float32
        )

    scores = mm(keys_new, qt_ref[...])
    key_pos = lax.broadcasted_iota(jnp.int32, (rows, columns), 0)
    query_pos = lax.broadcasted_iota(jnp.int32, (rows, columns), 1) % rows
    scores = jnp.where(key_pos <= query_pos, scores, neg_large)
    top = jnp.max(scores, axis=0, keepdims=True)
    weights = jnp.exp(scores - top)
    top_ref[...] = top
    total_ref[...] = jnp.sum(weights, axis=0, keepdims=True)
    acc_ref[...] = weigh(values_new, weights.astype(jnp.bfloat16))

    def visit(block_idx, masked):
        start = pl.multiple_of(block_idx * key_block, key_block)
        scores = mm(kc_ref[0, pl.ds(start, key_block), :], qt_ref[...])
        if masked:
            place = start + lax.broadcasted_iota(jnp.int32, (key_block, columns), 0)
            first = length - WINDOW + 1 + lax.broadcasted_iota(jnp.int32, (1, columns), 1) % rows
            live = (place < length) & ((place < SINK) | (place >= first))
            scores = jnp.where(live, scores, neg_large)
        top_old = top_ref[...]
        top_new = jnp.maximum(top_old, jnp.max(scores, axis=0, keepdims=True))
        weights = jnp.exp(scores - top_new)
        factor = jnp.exp(top_old - top_new)
        top_ref[...] = top_new
        total_ref[...] = total_ref[...] * factor + jnp.sum(weights, axis=0, keepdims=True)
        acc_ref[...] = acc_ref[...] * factor + weigh(
            vc_ref[0, pl.ds(start, key_block), :], weights.astype(jnp.bfloat16)
        )

    blocks = (length + key_block - 1) // key_block
    low = jnp.minimum(
        (jnp.maximum(length + rows - WINDOW, 0) + key_block - 1) // key_block, blocks
    )
    high = jnp.maximum(low, length // key_block)

    def run(begin, end, masked):
        def step(block_idx, carried):
            visit(block_idx, masked)
            return carried

        lax.fori_loop(begin, end, step, 0)

    run(0, low, True)
    run(low, high, False)
    run(high, blocks, True)
    result = acc_ref[...] / total_ref[...]
    parts = []
    for h in range(heads):
        kv = h // share
        parts.append(result[kv * HD : (kv + 1) * HD, h * rows : (h + 1) * rows])
    heads_rows = jnp.concatenate(parts, axis=0).T.astype(jnp.bfloat16)
    out_ref[...] = mm(heads_rows, wo_ref[...]).astype(jnp.bfloat16)


def attend(past_len, tokens, gain, w_query, w_key, w_value, w_out, cache_keys, cache_values):
    requests, capacity, kv_width = cache_keys.shape
    group_rows, width = tokens.shape
    rows = group_rows // requests
    key_block = math.gcd(capacity, 512)
    columns = w_query.shape[1] // HD * rows

    def whole(array):
        return pl.BlockSpec(
            array.shape, lambda i, lens: (0,) * array.ndim, pipeline_mode=pl.Buffered(1)
        )

    gain = gain.reshape(1, width)
    cache_spec = pl.BlockSpec((1, capacity, kv_width), lambda i, lens: (i, 0, 0))
    row_spec = pl.BlockSpec((rows, width), lambda i, lens: (i, 0))
    return pl.pallas_call(
        functools.partial(attend_kernel, key_block),
        out_shape=jax.ShapeDtypeStruct((group_rows, width), jnp.bfloat16),
        grid_spec=pltpu.PrefetchScalarGridSpec(
            num_scalar_prefetch=1,
            grid=(requests,),
            in_specs=[row_spec]
            + [whole(a) for a in (gain, w_query, w_key, w_value, w_out)]
            + [cache_spec, cache_spec],
            out_specs=row_spec,
            scratch_shapes=[
                pltpu.VMEM((kv_width, columns), jnp.bfloat16),
                pltpu.VMEM((1, columns), jnp.float32),
                pltpu.VMEM((1, columns), jnp.float32),
                pltpu.VMEM((kv_width, columns), jnp.float32),
            ],
        ),
        compiler_params=pltpu.CompilerParams(vmem_limit_bytes=48 << 20),
        name="attend",
    )(past_len, tokens, gain, w_query, w_key, w_value, w_out, cache_keys, cache_values)


def gate_kernel(attn_ref, tok_ref, gain_ref, router_ref, chosen_ref, stream_ref, ext_ref):
    width = tok_ref.shape[1]
    stream = tok_ref[...].astype(jnp.float32) + attn_ref[...].astype(jnp.float32)
    stream_ref[...] = stream
    moe_in = rms_scale(stream, gain_ref[...]).astype(jnp.bfloat16)
    ext_ref[:, :width] = moe_in
    logits = mm(moe_in, router_ref[...])
    chosen = chosen_ref[...] > 0.0
    top = jnp.max(jnp.where(chosen, logits, neg_large), axis=-1, keepdims=True)
    weights = jnp.where(chosen, jnp.exp(jnp.where(chosen, logits, top) - top), 0.0)
    gates = weights / (0.5 * jnp.sum(weights, axis=-1, keepdims=True))
    half = gates.shape[1] // 2
    coarse = gates.astype(jnp.bfloat16).astype(jnp.float32)
    lane = lax.broadcasted_iota(jnp.int32, gates.shape, 1)
    ext_ref[:, width:] = jnp.where(lane < half, coarse, gates - coarse).astype(jnp.bfloat16)


def gate_rows(attn_rows, rows_mine, gain, router2, chosen2):
    rows, width = rows_mine.shape
    return pl.pallas_call(
        gate_kernel,
        out_shape=(
            jax.ShapeDtypeStruct((rows, width), jnp.float32),
            jax.ShapeDtypeStruct((rows, width + router2.shape[1]), jnp.bfloat16),
        ),
        name="gate_rows",
    )(attn_rows, rows_mine, gain.reshape(1, width), router2, chosen2)


def experts_kernel(
    span, me_ref, ext_ref, win_ref, wout_ref, out_ref, rank_ref, rank_t_ref, acc_ref
):
    s = pl.program_id(0)
    slots = pl.num_programs(0)
    rows, wide = ext_ref.shape
    width = acc_ref.shape[1]
    extra = wide - width
    ff_width = wout_ref.shape[1]
    first = me_ref[0] * slots

    def pick_slot(shape, dim_from, dim_to, offset):
        source = lax.broadcasted_iota(jnp.int32, shape, dim_from) % (extra // 2)
        target = lax.broadcasted_iota(jnp.int32, shape, dim_to)
        return source == target + offset

    @pl.when(s == 0)
    def _():
        choose = pick_slot((extra, 128), 0, 1, first) & (
            lax.broadcasted_iota(jnp.int32, (extra, 128), 1) < slots
        )
        choose = jnp.where(choose, 1.0, 0.0).astype(jnp.bfloat16)
        before = jnp.where(
            lax.broadcasted_iota(jnp.int32, (span, span), 1)
            < lax.broadcasted_iota(jnp.int32, (span, span), 0),
            1.0,
            0.0,
        ).astype(jnp.bfloat16)
        seen = jnp.zeros((1, 128), jnp.float32)
        for part in range(rows // span):
            here = slice(part * span, (part + 1) * span)
            used = mm(ext_ref[here, width:], choose) > 0.0
            ones = jnp.where(used, 1.0, 0.0)
            rank = mm(before, ones.astype(jnp.bfloat16)) + seen
            rank = jnp.where(used, rank, -1.0)
            seen = seen + jnp.sum(ones, axis=0, keepdims=True)
            rank_ref[here, :] = rank
            rank_t_ref[:, here] = rank.T[: rank_t_ref.shape[0], :]
        acc_ref[...] = jnp.zeros_like(acc_ref)

    rank_row = rank_t_ref[pl.ds(s, 1), :]
    count = jnp.max(rank_row).astype(jnp.int32) + 1
    chunk = math.gcd(rows, 512)
    tile_rows = 256 if rows <= MOST_ROWS else 64

    def tile(index, carried):
        base = (index * tile_rows).astype(jnp.float32)
        wanted = base + lax.broadcasted_iota(jnp.int32, (tile_rows, rows), 0).astype(jnp.float32)
        select = jnp.where(wanted == rank_row, 1.0, 0.0).astype(jnp.bfloat16)
        taken = mm(select, ext_ref[...])
        moe_in = taken[:, :width].astype(jnp.bfloat16)
        lane = lax.broadcasted_iota(jnp.int32, (tile_rows, extra), 1) % (extra // 2)
        mine = lane == first + s
        gate = jnp.sum(jnp.where(mine, taken[:, width:], 0.0), axis=1, keepdims=True)
        gate_up = mm(moe_in, win_ref[0])
        g = gate_up[:, :ff_width]
        activation = (g / (1.0 + jnp.exp(-g)) * gate_up[:, ff_width:]).astype(jnp.bfloat16)
        produced = (mm(activation, wout_ref[0]) * gate).astype(jnp.bfloat16)
        for part in range(rows // chunk):
            here = slice(part * chunk, (part + 1) * chunk)
            lane_id = lax.broadcasted_iota(jnp.int32, (chunk, 128), 1)
            column = jnp.sum(
                jnp.where(lane_id == s, rank_ref[here, :], 0.0), axis=1, keepdims=True
            )
            place = base + lax.broadcasted_iota(jnp.int32, (chunk, tile_rows), 1).astype(jnp.float32)
            spread = jnp.where(place == column, 1.0, 0.0).astype(jnp.bfloat16)
            acc_ref[here, :] = acc_ref[here, :] + mm(spread, produced)
        return carried

    lax.fori_loop(0, (count + tile_rows - 1) // tile_rows, tile, 0)

    @pl.when(s == slots - 1)
    def _():
        out_ref[...] = acc_ref[...].astype(jnp.bfloat16)


def run_experts(me, gathered, expert_in, expert_out, span):
    rows, wide = gathered.shape
    slots, width, double = expert_in.shape
    ff_width = expert_out.shape[1]
    return pl.pallas_call(
        functools.partial(experts_kernel, span),
        out_shape=jax.ShapeDtypeStruct((rows, width), jnp.bfloat16),
        grid_spec=pltpu.PrefetchScalarGridSpec(
            num_scalar_prefetch=1,
            grid=(slots,),
            in_specs=[
                pl.BlockSpec((rows, wide), lambda i, me: (0, 0), pipeline_mode=pl.Buffered(1)),
                pl.BlockSpec((1, width, double), lambda i, me: (i, 0, 0)),
                pl.BlockSpec((1, ff_width, width), lambda i, me: (i, 0, 0)),
            ],
            out_specs=pl.BlockSpec((rows, width), lambda i, me: (0, 0), pipeline_mode=pl.Buffered(1)),
            scratch_shapes=[
                pltpu.VMEM((rows, 128), jnp.float32),
                pltpu.VMEM((-(-slots // 8) * 8, rows), jnp.float32),
                pltpu.VMEM((rows, width), jnp.float32),
            ],
        ),
        compiler_params=pltpu.CompilerParams(vmem_limit_bytes=64000 << 10),
        name="run_experts",
    )(me, gathered, expert_in, expert_out)


def choose_slots(slot_owner, routes, split_pick):
    slot_ids = jnp.arange(slot_owner.shape[0], dtype=jnp.int32)
    same_owner = slot_owner[:, None] == slot_owner[None, :]
    slot_rank = jnp.sum(
        (same_owner & (slot_ids[None, :] < slot_ids[:, None])).astype(jnp.int32), axis=1
    )
    replicas = jnp.sum(same_owner.astype(jnp.int32), axis=1)
    hits = (slot_owner[None, None, :] == routes[:, :, None]) & (
        slot_rank[None, None, :] == split_pick[:, :, None] % replicas[None, None, :]
    )
    return jnp.any(hits, axis=1).astype(jnp.float32)


def shards(
    tokens,
    past_len,
    cache_keys,
    cache_values,
    attn_gain,
    w_query,
    w_key,
    w_value,
    w_out,
    moe_gain,
    router,
    expert_in,
    expert_out,
    final_gain,
    slot_owner,
    routes,
    split_pick,
):
    chosen = choose_slots(slot_owner, routes, split_pick)
    chosen2 = jnp.concatenate([chosen, chosen], axis=1)
    owner2 = jnp.concatenate([slot_owner, slot_owner])
    pick = owner2[None, :] == jnp.arange(router.shape[1], dtype=jnp.int32)[:, None]
    router2 = mm(router, pick.astype(jnp.bfloat16)).astype(jnp.bfloat16)
    projected = attend(
        past_len, tokens, attn_gain, w_query, w_key, w_value, w_out, cache_keys, cache_values
    )
    tok_dev = tokens.shape[0] // lax.axis_size("dp")
    attn_rows = lax.psum_scatter(projected, "dp", scatter_dimension=0, tiled=True)
    rows_mine = lax.dynamic_slice_in_dim(tokens, lax.axis_index("dp") * tok_dev, tok_dev, 0)
    stream, extended = gate_rows(attn_rows, rows_mine, moe_gain, router2, chosen2)
    gathered = lax.all_gather(extended, "expert", axis=0, tiled=True)
    me = lax.axis_index("expert").astype(jnp.int32).reshape(1)
    partial = run_experts(me, gathered, expert_in, expert_out, tok_dev)
    mixed = lax.psum_scatter(partial, "expert", scatter_dimension=0, tiled=True)
    combined = stream + mixed.astype(jnp.float32)
    return rms_scale(combined, final_gain).astype(jnp.bfloat16)


def solution(mesh):
    return jax.shard_map(
        shards,
        mesh=mesh,
        in_specs=(
            P("expert", None),
            P("expert"),
            P("expert", None, "dp"),
            P("expert", None, "dp"),
            P(),
            P(None, "dp"),
            P(None, "dp"),
            P(None, "dp"),
            P("dp", None),
            P(),
            P(),
            P("expert", None, None),
            P("expert", None, None),
            P(),
            P(),
            P(("expert", "dp"), None),
            P(("expert", "dp"), None),
        ),
        out_specs=P(("expert", "dp"), None),
        check_vma=False,
    )
```

time: 598 us -> 217 us (0.36)
  blocking collectives: 179 us -> 0 us
  matrix products: 83 us -> 1.09 us
  Pallas kernels: 0 us -> 73.1 us
  waiting for transfers between devices: 186 us -> 114 us
  local copies, waits for them, and re-layouts: 64.4 us -> 8.42 us
  other arithmetic: 60.6 us -> 6.66 us
    all_to_all x1 -> x0, blocking collectives: 179 us -> none  [shards(): lax.all_to_all(outgoing, 'expert', split_axis=0, concat_axis=0, tiled=True)]
    all_to_all x1 -> x0, waiting for transfers between devices: 172 us -> none  [shards(): lax.all_to_all(produced, 'expert', split_axis=0, concat_axis=0, tiled=True)]
    dot_general x27 -> x1, matrix products: 83 us -> 1.09 us  [mm(): return jnp.dot(a, b, preferred_element_type=jnp.float32)]
    pallas_call x0 -> x3, Pallas kernels: none -> 73.1 us  [the longest x1 40.2 us: run_experts(): pl.pallas_call(functools.partial(experts_kernel, span), out_shape=jax.Sha...]
    reduce_scatter x1 -> x2, waiting for transfers between devices: 14.2 us -> 73.6 us  [the longest x1 41.6 us: shards(): mixed = lax.psum_scatter(partial, 'expert', scatter_dimension=0, tiled=True)]
    all_gather x0 -> x1, waiting for transfers between devices: none -> 40.4 us  [shards(): gathered = lax.all_gather(extended, 'expert', axis=0, tiled=True)]
    reduce_sum x17 -> x1, other arithmetic: 21.7 us -> 0.18 us  [choose_slots(): jnp.sum((same_owner & (slot_ids[None, :] < slot_ids[:, None])).astype(jnp...]
    scatter x1 -> x0, local copies, waits for them, and re-layouts: 20.7 us -> none  [shards(): outgoing = jnp.zeros((slot_total * most_rows, width), jnp.bfloat16).at[lo...]
  transfers between devices with their start and end apart: 2 -> 3, of which waited for: 2 -> 3; matrix products, arithmetic and copies ran while one was open for 3% -> 3% of each run, Pallas kernels for 0% -> 0%
where the time goes in v1:
time: 217 us
  waiting for transfers between devices  114 us (53%)
  Pallas kernels  73.1 us (34%)
  between operations  13.2 us (6%)
  local copies, waits for them, and re-layouts  8.42 us (4%)
  other arithmetic  6.66 us (3%)
    reduce_scatter x1, waiting for transfers between devices, shards(): mixed = lax.psum_scatter(partial, 'expert', scatter_dimension=0, tiled=True)  41.6 us
    all_gather x1, waiting for transfers between devices, shards(): gathered = lax.all_gather(extended, 'expert', axis=0, tiled=True)  40.4 us
    pallas_call x1, Pallas kernels, run_experts(): pl.pallas_call(functools.partial(experts_kernel, span), out_shape=jax.Sha...  40.2 us
    reduce_scatter x1, waiting for transfers between devices, shards(): lax.psum_scatter(projected, 'dp', scatter_dimension=0, tiled=True)  32 us
    pallas_call x1, Pallas kernels, attend(): pl.pallas_call(functools.partial(attend_kernel, key_block), out_shape=jax...  30.4 us
    unnamed x24, local copies, waits for them, and re-layouts  5.21 us
  transfers between devices with their start and end apart: 3, of which 3 were waited for; matrix products, arithmetic and copies ran while one was open for 3% of the time, Pallas kernels for 0%

profile of v1, /device:TPU:0, one launch (start us, length us, event | category | flops | bytes accessed | tf_op | source)
XLA Modules:
  0.0 216.7 jit_solution(5899643952209599987)
XLA Ops:
  6.5 0.0 copy-start
  6.5 0.0 reduce-scatter.3.cloned.1.call-start
  6.5 0.7 reshape.35.gain_ref
  7.3 0.0 copy-start.1
  7.3 1.3 copy-done.1
  8.5 0.0 copy-start.2
  8.6 1.3 copy-done.2
  9.8 0.0 copy-start.3
  9.8 1.0 copy-done.3
  10.8 0.0 copy-start.4
  10.8 1.0 copy-done.4
  11.8 0.0 copy-start.5
  11.8 0.7 copy-done.5
  12.5 0.0 copy-start.8
  12.5 0.0 copy-start.9
  12.5 0.0 copy-start.10
  12.5 0.0 copy-start.11
  12.5 30.4 %attend.1 = bf16[512,1536]{1,0:T(8,128)(2,1)} custom-call(s32[4]{0:T(128)S(1)} %copy-done.5, bf16[512,1536]{1,0:T(8,128)(2,1)} %tok_ref.1, f32[1,1536]{1,0:T(1,128)S(1)} %reshape.35.gain_ref, bf16[1536,384]{1,0:T(8,128)(2,1)S(1)} %copy-done.1, bf16[1536,128]{1,0:T(8,128)(2,1)S(1)} %copy-done.3, bf16[1536,128]{1,0:T(8,128)(2,1)S(1)} %copy-done.4, ...), custom_call_target="tpu_custom_call" | custom-call | tf_op jit(solution)/shard_map/attend/pallas_call | solution.py:123
  42.8 0.0 reduce-scatter.3.cloned.1.call-update
  42.9 0.0 all-gather.2.cloned.1.call-start
  42.9 0.0 copy-done.8
  42.9 0.6 reshape.36.gain_ref
  43.5 0.0 copy-done.9
  43.5 0.2 convert_reduce_fusion
  43.7 0.0 copy-done.10
  43.7 0.0 copy-done.11
  43.7 2.6 %fusion.5 = pred[128,64]{0,1:T(8,128)(4,1)S(1)} fusion(s32[64]{0:T(128)S(1)} %compare_select_fusion, s32[128,8]{0,1:T(8,128)S(1)} %copy-done.10, s32[64]{0:T(128)S(1)} %get-tuple-element.9, s32[128,8]{0,1:T(8,128)S(1)} %copy-done.11, s32[64]{0:T(128)S(1)} %copy-done.9, pred[64]{0:T(512)(128)(4,1)S(1)} %broadcast_compare_fusion), kind=kLoop, calls=%fused_computation.13 | loop fusion | flops 712704 | bytes 17216 | tf_op jit(solution)/shard_map/reduce_or | solution.py:287
  46.4 0.1 copy.22
  46.5 0.1 pad_add_fusion
  46.6 0.7 add_convert_fusion.chosen_ref
  47.3 0.0 copy-done
  47.3 1.1 fusion.router_ref
  48.4 1.8 constant_dynamic-slice_fusion.tok_ref
  50.1 32.0 %reduce-scatter.3.cloned.1.call-done.attn_ref = bf16[128,1536]{1,0:T(8,128)(2,1)} async-done(((bf16[512,1536]{1,0:T(8,128)(2,1)}), bf16[128,1536]{1,0:T(8,128)(2,1)}) %reduce-scatter.3.cloned.1.call-update) | async-done | bytes 393232 | tf_op jit(solution)/shard_map/reduce_scatter | solution.py:318
  82.2 2.6 %gate_rows.1 = (f32[128,1536]{1,0:T(8,128)}, bf16[128,1664]{1,0:T(8,128)(2,1)}) custom-call(bf16[128,1536]{1,0:T(8,128)(2,1)} %reduce-scatter.3.cloned.1.call-done.attn_ref, bf16[128,1536]{1,0:T(8,128)(2,1)} %constant_dynamic-slice_fusion.tok_ref, f32[1,1536]{1,0:T(1,128)} %reshape.36.gain_ref, bf16[1536,128]{1,0:T(8,128)(2,1)} %fusion.router_ref, ...), custom_call_target="tpu_custom_call" | custom-call | tf_op jit(solution)/shard_map/gate_rows/pallas_call | solution.py:164
  84.8 0.0 all-gather.2.cloned.1.call-update
  84.8 0.2 reduce-scatter.5.cloned.1.call-start
  85.0 40.4 %all-gather.2.cloned.1.call-done.ext_ref = bf16[1024,1664]{1,0:T(8,128)(2,1)} async-done(((bf16[128,1664]{1,0:T(8,128)(2,1)}), bf16[1024,1664]{1,0:T(8,128)(2,1)}) %all-gather.2.cloned.1.call-update) | async-done | bytes 3407888 | tf_op jit(solution)/shard_map/all_gather | solution.py:321
  125.4 40.2 %run_experts.1 = bf16[1024,1536]{1,0:T(8,128)(2,1)} custom-call(s32[1]{0:T(128)} %bitcast.1.me_ref, bf16[1024,1664]{1,0:T(8,128)(2,1)} %all-gather.2.cloned.1.call-done.ext_ref, bf16[8,1536,1024]{2,1,0:T(8,128)(2,1)} %win_ref.1, bf16[8,512,1536]{2,1,0:T(8,128)(2,1)} %wout_ref.1), custom_call_target="tpu_custom_call" | custom-call | tf_op jit(solution)/shard_map/run_experts/pallas_call | solution.py:254
  165.5 0.0 copy-start.6
  165.5 0.0 copy-start.7
  165.5 0.0 reduce-scatter.5.cloned.1.call-update
  165.6 41.6 %reduce-scatter.5.cloned.1.call-done = bf16[128,1536]{1,0:T(8,128)(2,1)} async-done(((bf16[1024,1536]{1,0:T(8,128)(2,1)}), bf16[128,1536]{1,0:T(8,128)(2,1)}) %reduce-scatter.5.cloned.1.call-update) | async-done | bytes 393232 | tf_op jit(solution)/shard_map/reduce_scatter | solution.py:324
  207.1 0.0 copy-done.6
  207.1 1.2 multiply_reduce_fusion
  208.3 0.0 copy-done.7
  208.3 1.9 multiply_convert_fusion
  (3 shorter events, 0.0 us)
Async XLA Ops:
  6.5 40.7 %copy-start = (bf16[1536,40]{0,1:T(8,128)(2,1)S(1)}, bf16[1536,40]{0,1:T(8,128)(2,1)}, u32[]{:S(2)}) copy-start(bf16[1536,40]{0,1:T(8,128)(2,1)} %param.27) | copy-start | bytes 368644
  6.5 75.6 %reduce-scatter.3.cloned.1.call-start = ((), (), s32[]{:S(2)}) async-start(), calls=%async_computation.2 | async-start | bytes 1966080 | tf_op jit(solution)/shard_map/reduce_scatter | solution.py:318
  7.3 1.3 copy-start.1
  8.5 1.3 copy-start.2
  9.8 1.0 copy-start.3
  10.8 1.0 copy-start.4
  11.8 0.7 copy-start.5
  12.5 30.4 %copy-start.8 = (f32[1536]{0:T(1024)S(1)}, f32[1536]{0:T(1024)}, u32[]{:S(2)}) copy-start(f32[1536]{0:T(1024)} %param.26) | copy-start | bytes 18436
  12.5 31.0 %copy-start.9 = (s32[64]{0:T(128)S(1)}, s32[64]{0:T(128)}, u32[]{:S(2)}) copy-start(s32[64]{0:T(128)} %param.31) | copy-start | bytes 772
  12.5 31.2 %copy-start.10 = (s32[128,8]{0,1:T(8,128)S(1)}, s32[128,8]{0,1:T(8,128)}, u32[]{:S(2)}) copy-start(s32[128,8]{0,1:T(8,128)} %param.33) | copy-start | bytes 12292
  12.5 31.3 %copy-start.11 = (s32[128,8]{0,1:T(8,128)S(1)}, s32[128,8]{0,1:T(8,128)}, u32[]{:S(2)}) copy-start(s32[128,8]{0,1:T(8,128)} %param.32) | copy-start | bytes 12292
  42.9 82.5 %all-gather.2.cloned.1.call-start = ((), (), s32[]{:S(2)}) async-start(), calls=%async_computation.3 | async-start | bytes 3833856 | tf_op jit(solution)/shard_map/all_gather | solution.py:321
  84.8 122.3 %reduce-scatter.5.cloned.1.call-start = ((), (), s32[]{:S(2)}) async-start(), calls=%async_computation.4 | async-start | bytes 3538944 | tf_op jit(solution)/shard_map/reduce_scatter | solution.py:324
  165.5 41.6 %copy-start.6 = (f32[128,1536]{1,0:T(8,128)S(1)}, f32[128,1536]{1,0:T(8,128)}, u32[]{:S(2)}) copy-start(f32[128,1536]{1,0:T(8,128)} %get-tuple-element.7) | copy-start | bytes 2359300
  165.5 42.8 %copy-start.7 = (f32[1536]{0:T(1024)S(1)}, f32[1536]{0:T(1024)}, u32[]{:S(2)}) copy-start(f32[1536]{0:T(1024)} %param.30) | copy-start | bytes 18436
Sparse Core Ops, SparseCore 0:
  43.0 39.1 reduce-scatter.2
  84.9 40.4 all-gather.1
  165.7 41.3 reduce-scatter.4

commit v2 on v1

--- a/solution.py
+++ b/solution.py
@@ -12,6 +12,7 @@
 SINK = 4
 WINDOW = 4096
 MOST_ROWS = 2048
+CHUNKS = 2
 
 epsilon = 1e-05
 neg_large = -1e30
@@ -29,8 +30,9 @@
 
 def attend_kernel(
     key_block, len_ref, tok_ref, gain_ref, wq_ref, wk_ref, wv_ref, wo_ref, kc_ref, vc_ref,
-    out_ref, qt_ref, top_ref, total_ref, acc_ref,
+    *refs,
 ):
+    out_refs, (qt_ref, top_ref, total_ref, acc_ref) = refs[:-4], refs[-4:]
     length = len_ref[pl.program_id(0)]
     rows = tok_ref.shape[0]
     heads = wq_ref.shape[1] // HD
@@ -102,7 +104,10 @@
         kv = h // share
         parts.append(result[kv * HD : (kv + 1) * HD, h * rows : (h + 1) * rows])
     heads_rows = jnp.concatenate(parts, axis=0).T.astype(jnp.bfloat16)
-    out_ref[...] = mm(heads_rows, wo_ref[...]).astype(jnp.bfloat16)
+    projected = mm(heads_rows, wo_ref[...]).astype(jnp.bfloat16)
+    part = rows // len(out_refs)
+    for index, out_ref in enumerate(out_refs):
+        out_ref[...] = projected[index * part : (index + 1) * part, :]
 
 
 def attend(past_len, tokens, gain, w_query, w_key, w_value, w_out, cache_keys, cache_values):
@@ -122,14 +127,14 @@
     row_spec = pl.BlockSpec((rows, width), lambda i, lens: (i, 0))
     return pl.pallas_call(
         functools.partial(attend_kernel, key_block),
-        out_shape=jax.ShapeDtypeStruct((group_rows, width), jnp.bfloat16),
+        out_shape=[jax.ShapeDtypeStruct((group_rows // CHUNKS, width), jnp.bfloat16)] * CHUNKS,
         grid_spec=pltpu.PrefetchScalarGridSpec(
             num_scalar_prefetch=1,
             grid=(requests,),
             in_specs=[row_spec]
             + [whole(a) for a in (gain, w_query, w_key, w_value, w_out)]
             + [cache_spec, cache_spec],
-            out_specs=row_spec,
+            out_specs=[pl.BlockSpec((rows // CHUNKS, width), lambda i, lens: (i, 0))] * CHUNKS,
             scratch_shapes=[
                 pltpu.VMEM((kv_width, columns), jnp.bfloat16),
                 pltpu.VMEM((1, columns), jnp.float32),
@@ -138,6 +143,11 @@
             ],
         ),
         compiler_params=pltpu.CompilerParams(vmem_limit_bytes=48 << 20),
+        cost_estimate=pl.CostEstimate(
+            flops=8 * cache_keys.size * columns,
+            bytes_accessed=cache_keys.size * 4,
+            transcendentals=0,
+        ),
         name="attend",
     )(past_len, tokens, gain, w_query, w_key, w_value, w_out, cache_keys, cache_values)
 
@@ -214,7 +224,7 @@
     rank_row = rank_t_ref[pl.ds(s, 1), :]
     count = jnp.max(rank_row).astype(jnp.int32) + 1
     chunk = math.gcd(rows, 512)
-    tile_rows = 256 if rows <= MOST_ROWS else 64
+    tile_rows = 128 if rows <= MOST_ROWS else 64
 
     def tile(index, carried):
         base = (index * tile_rows).astype(jnp.float32)
@@ -247,8 +257,9 @@
         out_ref[...] = acc_ref[...].astype(jnp.bfloat16)
 
 
-def run_experts(me, gathered, expert_in, expert_out, span):
+def run_experts(me, gathered, expert_in, expert_out):
     rows, wide = gathered.shape
+    span = math.gcd(rows, 256)
     slots, width, double = expert_in.shape
     ff_width = expert_out.shape[1]
     return pl.pallas_call(
@@ -270,8 +281,32 @@
             ],
         ),
         compiler_params=pltpu.CompilerParams(vmem_limit_bytes=64000 << 10),
+        cost_estimate=pl.CostEstimate(
+            flops=16 * rows * width * ff_width * 8,
+            bytes_accessed=expert_in.size * 2 + expert_out.size * 2 + rows * (wide + width) * 2,
+            transcendentals=0,
+        ),
         name="run_experts",
     )(me, gathered, expert_in, expert_out)
+
+
+def finish_kernel(*refs):
+    gain_ref, out_ref = refs[-2:]
+    part = refs[0].shape[0]
+    for index in range(CHUNKS):
+        combined = refs[index][...] + refs[CHUNKS + index][...].astype(jnp.float32)
+        out_ref[index * part : (index + 1) * part, :] = rms_scale(combined, gain_ref[...]).astype(
+            jnp.bfloat16
+        )
+
+
+def finish(streams, mixes, gain):
+    part, width = streams[0].shape
+    return pl.pallas_call(
+        finish_kernel,
+        out_shape=jax.ShapeDtypeStruct((part * CHUNKS, width), jnp.bfloat16),
+        name="finish",
+    )(*streams, *mixes, gain.reshape(1, width))
 
 
 def choose_slots(slot_owner, routes, split_pick):
@@ -315,15 +350,21 @@
         past_len, tokens, attn_gain, w_query, w_key, w_value, w_out, cache_keys, cache_values
     )
     tok_dev = tokens.shape[0] // lax.axis_size("dp")
-    attn_rows = lax.psum_scatter(projected, "dp", scatter_dimension=0, tiled=True)
-    rows_mine = lax.dynamic_slice_in_dim(tokens, lax.axis_index("dp") * tok_dev, tok_dev, 0)
-    stream, extended = gate_rows(attn_rows, rows_mine, moe_gain, router2, chosen2)
-    gathered = lax.all_gather(extended, "expert", axis=0, tiled=True)
+    part = tok_dev // CHUNKS
     me = lax.axis_index("expert").astype(jnp.int32).reshape(1)
-    partial = run_experts(me, gathered, expert_in, expert_out, tok_dev)
-    mixed = lax.psum_scatter(partial, "expert", scatter_dimension=0, tiled=True)
-    combined = stream + mixed.astype(jnp.float32)
-    return rms_scale(combined, final_gain).astype(jnp.bfloat16)
+    streams, mixes = [], []
+    for index in range(CHUNKS):
+        attn_rows = lax.psum_scatter(projected[index], "dp", scatter_dimension=0, tiled=True)
+        begin = lax.axis_index("dp") * tok_dev + index * part
+        rows_mine = lax.dynamic_slice_in_dim(tokens, begin, part, 0)
+        here = slice(index * part, (index + 1) * part)
+        stream, extended = gate_rows(attn_rows, rows_mine, moe_gain, router2, chosen2[here])
+        gathered = lax.all_gather(extended, "expert", axis=0, tiled=True)
+        partial = run_experts(me, gathered, expert_in, expert_out)
+        mixed = lax.psum_scatter(partial, "expert", scatter_dimension=0, tiled=True)
+        streams.append(stream)
+        mixes.append(mixed)
+    return finish(streams, mixes, final_gain)
 
 
 def solution(mesh):

time: 217 us -> 239 us (1.10)
  waiting for transfers between devices: 114 us -> 136 us
  other arithmetic: 6.66 us -> 2.97 us
  Pallas kernels: 73.1 us -> 75.8 us
    reduce_scatter x1 -> x2, waiting for transfers between devices: 32 us -> 55.6 us  [shards(): lax.psum_scatter(projected[index], 'dp', scatter_dimension=0, tiled=True)]
    all_gather x1 -> x2, waiting for transfers between devices: 40.4 us -> 31.1 us  [shards(): gathered = lax.all_gather(extended, 'expert', axis=0, tiled=True)]
    reduce_scatter x1 -> x2, waiting for transfers between devices: 41.6 us -> 49 us  [shards(): mixed = lax.psum_scatter(partial, 'expert', scatter_dimension=0, tiled=True)]
    pallas_call x1 -> x2, Pallas kernels: 40.2 us -> 41.7 us  [run_experts(): pl.pallas_call(functools.partial(experts_kernel, span), out_shape=jax.Sha...]
    pallas_call x1 -> x2, Pallas kernels: 30.4 us -> 29.4 us  [the longest x1 27.2 us: attend(): pl.pallas_call(functools.partial(attend_kernel, key_block), out_shape=[ja...]
    unnamed x24 -> x22, local copies, waits for them, and re-layouts: 5.21 us -> 5.21 us
  transfers between devices with their start and end apart: 3 -> 6, of which waited for: 3 -> 6; matrix products, arithmetic and copies ran while one was open for 3% -> 3% of each run, Pallas kernels for 0% -> 19%
where the time goes in v2:
time: 239 us; the launch traced here: 240 us
  waiting for transfers between devices  136 us (57%)
  Pallas kernels  75.8 us (32%)
  between operations  13.6 us (6%)
  local copies, waits for them, and re-layouts  9.72 us (4%)
  other arithmetic  2.97 us (1%)
    reduce_scatter x2, waiting for transfers between devices, shards(): lax.psum_scatter(projected[index], 'dp', scatter_dimension=0, tiled=True)  55.6 us
    reduce_scatter x2, waiting for transfers between devices, shards(): mixed = lax.psum_scatter(partial, 'expert', scatter_dimension=0, tiled=True)  49 us
    pallas_call x2, Pallas kernels, run_experts(): pl.pallas_call(functools.partial(experts_kernel, span), out_shape=jax.Sha...  41.7 us
    all_gather x2, waiting for transfers between devices, shards(): gathered = lax.all_gather(extended, 'expert', axis=0, tiled=True)  31.1 us
    pallas_call x1, Pallas kernels, attend(): pl.pallas_call(functools.partial(attend_kernel, key_block), out_shape=[ja...  27.2 us
    unnamed x22, local copies, waits for them, and re-layouts  5.21 us
  transfers between devices with their start and end apart: 6, of which 6 were waited for; matrix products, arithmetic and copies ran while one was open for 3% of the time, Pallas kernels for 19%

profile of v2, /device:TPU:0, one launch (start us, length us, event | category | flops | bytes accessed | tf_op | source)
XLA Modules:
  0.0 239.8 jit_solution(14784913087331968881)
XLA Ops:
  6.5 0.0 copy-start
  6.5 0.0 reduce-scatter.5.cloned.1.call-start
  6.5 0.7 reshape.30.gain_ref
  7.3 0.0 copy-start.1
  7.3 1.3 copy-done.1
  8.5 0.0 copy-start.2
  8.6 1.3 copy-done.2
  9.8 0.0 copy-start.3
  9.8 1.0 copy-done.3
  10.8 0.0 copy-start.4
  10.8 1.0 copy-done.4
  11.8 0.0 copy-start.5
  11.8 0.7 copy-done.5
  12.5 0.0 copy-start.6
  12.5 0.0 copy-start.8
  12.5 0.0 copy-start.9
  12.5 0.0 copy-start.10
  12.5 27.2 %attend.1 = (bf16[256,1536]{1,0:T(8,128)(2,1)}, bf16[256,1536]{1,0:T(8,128)(2,1)}) custom-call(s32[4]{0:T(128)S(1)} %copy-done.5, bf16[512,1536]{1,0:T(8,128)(2,1)} %tok_ref.1, f32[1,1536]{1,0:T(1,128)S(1)} %reshape.30.gain_ref, bf16[1536,384]{1,0:T(8,128)(2,1)S(1)} %copy-done.1, bf16[1536,128]{1,0:T(8,128)(2,1)S(1)} %copy-done.3, ...), custom_call_target="tpu_custom_call" | custom-call | flops 14495514624 | bytes 9437184 | tf_op jit(solution)/shard_map/attend/pallas_call | solution.py:128
  39.7 0.0 reduce-scatter.5.cloned.1.call-update
  39.7 0.0 reduce-scatter.7.cloned.1.call-start
  39.8 0.7 reduce-scatter.7.cloned.1.call-update
  40.5 0.0 all-gather.3.cloned.1.call-start
  40.5 0.0 copy-done.6
  40.5 0.6 reshape.31.gain_ref
  41.1 0.0 copy-done.8
  41.1 0.2 convert_reduce_fusion
  41.3 0.0 copy-done.9
  41.4 0.0 copy-done.10
  41.4 2.6 %fusion.5 = pred[128,64]{0,1:T(8,128)(4,1)S(1)} fusion(s32[64]{0:T(128)S(1)} %compare_select_fusion, s32[128,8]{0,1:T(8,128)S(1)} %copy-done.9, s32[64]{0:T(128)S(1)} %get-tuple-element.17, s32[128,8]{0,1:T(8,128)S(1)} %copy-done.10, s32[64]{0:T(128)S(1)} %copy-done.8, pred[64]{0:T(512)(128)(4,1)S(1)} %broadcast_compare_fusion), kind=kLoop, calls=%fused_computation.10 | loop fusion | flops 712704 | bytes 17216 | tf_op jit(solution)/shard_map/reduce_or | solution.py:322
  44.0 0.1 copy.22
  44.1 0.1 pad_add_fusion
  44.2 0.1 add_convert_fusion
  44.3 0.6 fusion.8
  44.9 0.0 copy-done
  44.9 1.1 fusion.router_ref
  46.0 1.8 constant_dynamic-slice_fusion
  47.8 29.0 %reduce-scatter.5.cloned.1.call-done.attn_ref = bf16[64,1536]{1,0:T(8,128)(2,1)} async-done(((bf16[256,1536]{1,0:T(8,128)(2,1)}), bf16[64,1536]{1,0:T(8,128)(2,1)}) %reduce-scatter.5.cloned.1.call-update) | async-done | bytes 196624 | tf_op jit(solution)/shard_map/reduce_scatter | solution.py:357
  76.8 2.4 gate_rows.2
  79.2 0.0 all-gather.3.cloned.1.call-update
  79.2 0.0 all-gather.5.cloned.1.call-start
  79.3 26.6 %reduce-scatter.7.cloned.1.call-done.attn_ref = bf16[64,1536]{1,0:T(8,128)(2,1)} async-done(((bf16[256,1536]{1,0:T(8,128)(2,1)}), bf16[64,1536]{1,0:T(8,128)(2,1)}) %reduce-scatter.7.cloned.1.call-update) | async-done | bytes 196624 | tf_op jit(solution)/shard_map/reduce_scatter | solution.py:357
  105.9 2.3 gate_rows.3
  108.2 0.0 all-gather.5.cloned.1.call-update
  108.2 0.0 reduce-scatter.9.cloned.1.call-start
  108.3 25.1 %all-gather.3.cloned.1.call-done.ext_ref = bf16[512,1664]{1,0:T(8,128)(2,1)} async-done(((bf16[64,1664]{1,0:T(8,128)(2,1)}), bf16[512,1664]{1,0:T(8,128)(2,1)}) %all-gather.3.cloned.1.call-update) | async-done | bytes 1703952 | tf_op jit(solution)/shard_map/all_gather | solution.py:362
  133.4 20.9 %run_experts.2 = bf16[512,1536]{1,0:T(8,128)(2,1)} custom-call(s32[1]{0:T(128)} %bitcast.1.me_ref, bf16[512,1664]{1,0:T(8,128)(2,1)} %all-gather.3.cloned.1.call-done.ext_ref, bf16[8,1536,1024]{2,1,0:T(8,128)(2,1)} %win_ref.3, bf16[8,512,1536]{2,1,0:T(8,128)(2,1)} %wout_ref.3), custom_call_target="tpu_custom_call" | custom-call | flops 51539607552 | bytes 41025536 | tf_op jit(solution)/shard_map/run_experts/pallas_call | solution.py:265
  154.3 0.0 reduce-scatter.9.cloned.1.call-update
  154.3 0.0 copy-start.7
  154.3 0.0 reduce-scatter.11.cloned.1.call-start
  154.3 6.0 %all-gather.5.cloned.1.call-done.ext_ref = bf16[512,1664]{1,0:T(8,128)(2,1)} async-done(((bf16[64,1664]{1,0:T(8,128)(2,1)}), bf16[512,1664]{1,0:T(8,128)(2,1)}) %all-gather.5.cloned.1.call-update) | async-done | bytes 1703952 | tf_op jit(solution)/shard_map/all_gather | solution.py:362
  160.3 20.8 %run_experts.3 = bf16[512,1536]{1,0:T(8,128)(2,1)} custom-call(s32[1]{0:T(128)} %bitcast.1.me_ref, bf16[512,1664]{1,0:T(8,128)(2,1)} %all-gather.5.cloned.1.call-done.ext_ref, bf16[8,1536,1024]{2,1,0:T(8,128)(2,1)} %win_ref.3, bf16[8,512,1536]{2,1,0:T(8,128)(2,1)} %wout_ref.3), custom_call_target="tpu_custom_call" | custom-call | flops 51539607552 | bytes 41025536 | tf_op jit(solution)/shard_map/run_experts/pallas_call | solution.py:265
  181.2 0.0 reduce-scatter.11.cloned.1.call-update
  181.2 0.0 copy-done.7
  181.2 0.6 reshape.33.refs_4_
  181.8 14.3 %reduce-scatter.9.cloned.1.call-done.refs_2_ = bf16[64,1536]{1,0:T(8,128)(2,1)} async-done(((bf16[512,1536]{1,0:T(8,128)(2,1)}), bf16[64,1536]{1,0:T(8,128)(2,1)}) %reduce-scatter.9.cloned.1.call-update) | async-done | bytes 196624 | tf_op jit(solution)/shard_map/reduce_scatter | solution.py:364
  196.1 34.7 %reduce-scatter.11.cloned.1.call-done.refs_3_ = bf16[64,1536]{1,0:T(8,128)(2,1)} async-done(((bf16[512,1536]{1,0:T(8,128)(2,1)}), bf16[64,1536]{1,0:T(8,128)(2,1)}) %reduce-scatter.11.cloned.1.call-update) | async-done | bytes 196624 | tf_op jit(solution)/shard_map/reduce_scatter | solution.py:364
  230.8 2.2 finish.1
  (2 shorter events, 0.0 us)
Async XLA Ops:
  6.5 38.4 %copy-start = (bf16[1536,40]{0,1:T(8,128)(2,1)S(1)}, bf16[1536,40]{0,1:T(8,128)(2,1)}, u32[]{:S(2)}) copy-start(bf16[1536,40]{0,1:T(8,128)(2,1)} %param.27) | copy-start | bytes 368644
  6.5 70.3 %reduce-scatter.5.cloned.1.call-start = ((), (), s32[]{:S(2)}) async-start(), calls=%async_computation.4 | async-start | bytes 983040 | tf_op jit(solution)/shard_map/reduce_scatter | solution.py:357
  7.3 1.3 copy-start.1
  8.5 1.3 copy-start.2
  9.8 1.0 copy-start.3
  10.8 1.0 copy-start.4
  11.8 0.7 copy-start.5
  12.5 28.1 %copy-start.6 = (f32[1536]{0:T(1024)S(1)}, f32[1536]{0:T(1024)}, u32[]{:S(2)}) copy-start(f32[1536]{0:T(1024)} %param.26) | copy-start | bytes 18436
  12.5 28.7 %copy-start.8 = (s32[64]{0:T(128)S(1)}, s32[64]{0:T(128)}, u32[]{:S(2)}) copy-start(s32[64]{0:T(128)} %param.31) | copy-start | bytes 772
  12.5 28.9 %copy-start.9 = (s32[128,8]{0,1:T(8,128)S(1)}, s32[128,8]{0,1:T(8,128)}, u32[]{:S(2)}) copy-start(s32[128,8]{0,1:T(8,128)} %param.33) | copy-start | bytes 12292
  12.5 28.9 %copy-start.10 = (s32[128,8]{0,1:T(8,128)S(1)}, s32[128,8]{0,1:T(8,128)}, u32[]{:S(2)}) copy-start(s32[128,8]{0,1:T(8,128)} %param.32) | copy-start | bytes 12292
  39.7 66.1 %reduce-scatter.7.cloned.1.call-start = ((), (), s32[]{:S(2)}) async-start(), calls=%async_computation.5 | async-start | bytes 983040 | tf_op jit(solution)/shard_map/reduce_scatter | solution.py:357
  40.5 92.9 %all-gather.3.cloned.1.call-start = ((), (), s32[]{:S(2)}) async-start(), calls=%async_computation.6 | async-start | bytes 1916928 | tf_op jit(solution)/shard_map/all_gather | solution.py:362
  79.2 81.1 %all-gather.5.cloned.1.call-start = ((), (), s32[]{:S(2)}) async-start(), calls=%async_computation.8 | async-start | bytes 1916928 | tf_op jit(solution)/shard_map/all_gather | solution.py:362
  108.2 87.9 %reduce-scatter.9.cloned.1.call-start = ((), (), s32[]{:S(2)}) async-start(), calls=%async_computation.7 | async-start | bytes 1769472 | tf_op jit(solution)/shard_map/reduce_scatter | solution.py:364
  154.3 26.9 %copy-start.7 = (f32[1536]{0:T(1024)S(1)}, f32[1536]{0:T(1024)}, u32[]{:S(2)}) copy-start(f32[1536]{0:T(1024)} %param.30) | copy-start | bytes 18436
  154.3 76.5 %reduce-scatter.11.cloned.1.call-start = ((), (), s32[]{:S(2)}) async-start(), calls=%async_computation.9 | async-start | bytes 1769472 | tf_op jit(solution)/shard_map/reduce_scatter | solution.py:364
Sparse Core Ops, SparseCore 0:
  39.8 36.9 reduce-scatter.4
  79.7 26.0 reduce-scatter.6
  107.5 25.8 all-gather.2
  134.9 25.3 all-gather.4
  162.5 33.5 reduce-scatter.8
  198.3 32.4 reduce-scatter.10

commit v3 on v1

--- a/solution.py
+++ b/solution.py
@@ -142,9 +142,75 @@
     )(past_len, tokens, gain, w_query, w_key, w_value, w_out, cache_keys, cache_values)
 
 
-def gate_kernel(attn_ref, tok_ref, gain_ref, router_ref, chosen_ref, stream_ref, ext_ref):
-    width = tok_ref.shape[1]
-    stream = tok_ref[...].astype(jnp.float32) + attn_ref[...].astype(jnp.float32)
+def start_if(cond, copy):
+    pl.when(cond)(copy.start)
+
+
+def greet(targets):
+    barrier = pltpu.get_barrier_semaphore()
+    total = 0
+    for cond, device in targets:
+
+        @pl.when(cond)
+        def _():
+            pl.semaphore_signal(
+                barrier, inc=1, device_id=device, device_id_type=pl.DeviceIdType.MESH
+            )
+
+        total = total + jnp.where(cond, 1, 0)
+    pl.semaphore_wait(barrier, total)
+
+
+def send(src, dst, send_sem, recv_sem, device):
+    return pltpu.make_async_remote_copy(
+        src_ref=src,
+        dst_ref=dst,
+        send_sem=send_sem,
+        recv_sem=recv_sem,
+        device_id=device,
+        device_id_type=pl.DeviceIdType.MESH,
+    )
+
+
+def exchange_kernel(
+    dp_size, chips, proj_ref, tok_ref, gain_ref, router_ref, chosen_ref,
+    stream_ref, all_ref,
+    mine_ref, got_ref, ext_ref,
+    tok_sem, own_sem, rs_send, rs_recv, up_send, up_recv, dn_send, dn_recv, sib_send, sib_recv,
+):
+    rows, wide = ext_ref.shape
+    width = mine_ref.shape[1]
+    dp, ex = lax.axis_index("dp"), lax.axis_index("expert")
+    chip, core = ex // 2, ex % 2
+    upper, lower = chip < chips - 1, chip > 0
+    true = chip >= 0
+    sibling = (dp, chip * 2 + 1 - core)
+    above = (dp, jnp.minimum(chip + 1, chips - 1) * 2 + core)
+    below = (dp, jnp.maximum(chip - 1, 0) * 2 + core)
+    load = pltpu.make_async_copy(tok_ref.at[pl.ds(dp * rows, rows)], mine_ref, tok_sem)
+    load.start()
+    greet(
+        [(true, (lax.rem(dp + k, dp_size), ex)) for k in range(1, dp_size)]
+        + [(true, sibling), (upper, above), (lower, below)]
+    )
+    copies = []
+    for k in range(1, dp_size):
+        peer = lax.rem(dp + k, dp_size)
+        copy = send(
+            proj_ref.at[pl.ds(peer * rows, rows)],
+            got_ref.at[k - 1],
+            rs_send.at[k - 1],
+            rs_recv.at[k - 1],
+            (peer, ex),
+        )
+        copy.start()
+        copies.append(copy)
+    load.wait()
+    attn = proj_ref[pl.ds(dp * rows, rows), :].astype(jnp.float32)
+    for k, copy in enumerate(copies):
+        copy.wait()
+        attn = attn + got_ref[k].astype(jnp.float32)
+    stream = mine_ref[...].astype(jnp.float32) + attn
     stream_ref[...] = stream
     moe_in = rms_scale(stream, gain_ref[...]).astype(jnp.bfloat16)
     ext_ref[:, :width] = moe_in
@@ -158,17 +224,183 @@
     lane = lax.broadcasted_iota(jnp.int32, gates.shape, 1)
     ext_ref[:, width:] = jnp.where(lane < half, coarse, gates - coarse).astype(jnp.bfloat16)
 
-
-def gate_rows(attn_rows, rows_mine, gain, router2, chosen2):
-    rows, width = rows_mine.shape
+    def block(chip_id, core_id):
+        bounded = jnp.clip(chip_id, 0, chips - 1)
+        return all_ref.at[pl.ds((bounded * 2 + core_id) * rows, rows)]
+
+    own = pltpu.make_async_copy(ext_ref, block(chip, core), own_sem)
+    own.start()
+
+    def hop(chip_id, src, sends, recvs, index, target):
+        return send(src, block(chip_id, core), sends.at[index], recvs.at[index], target)
+
+    waits = []
+    for s in range(chips):
+        if s < chips - 1:
+            for sign, edge, target, sends, recvs in (
+                (-1, upper, above, up_send, up_recv),
+                (1, lower, below, dn_send, dn_recv),
+            ):
+                origin = chip + sign * s
+                cond = edge & (origin >= 0) & (origin < chips)
+                copy = hop(origin, ext_ref if s == 0 else block(origin, core), sends, recvs, s, target)
+                start_if(cond, copy)
+                waits.append((cond, copy))
+        for sign, index in ((-1, s), (1, chips - 1 + s)):
+            origin = chip + sign * s
+            if s == 0 and sign == 1:
+                continue
+            cond = (origin >= 0) & (origin < chips)
+            copy = hop(origin, ext_ref if s == 0 else block(origin, core), sib_send, sib_recv, index, sibling)
+            start_if(cond, copy)
+            waits.append((cond, copy))
+        if s < chips - 1:
+            for sign, target, sends, recvs in (
+                (-1, above, up_send, up_recv),
+                (1, below, dn_send, dn_recv),
+            ):
+                origin = chip + sign * (s + 1)
+                cond = (origin >= 0) & (origin < chips)
+                copy = hop(origin, ext_ref, sends, recvs, s, target)
+                pl.when(cond)(copy.wait_recv)
+    for cond, copy in waits:
+        pl.when(cond)(copy.wait_send)
+    for s in range(chips):
+        for sign, index in ((-1, s), (1, chips - 1 + s)):
+            if s == 0 and sign == 1:
+                continue
+            origin = chip + sign * s
+            copy = send(ext_ref, block(origin, 1 - core), sib_send.at[index], sib_recv.at[index], sibling)
+            pl.when((origin >= 0) & (origin < chips))(copy.wait_recv)
+    own.wait()
+
+
+def exchange(projected, tokens, gain, router2, chosen2, dp_size, ex_size):
+    group_rows, width = tokens.shape
+    rows = group_rows // dp_size
+    wide = width + router2.shape[1]
+    chips = ex_size // 2
+    dma = pltpu.SemaphoreType.DMA
+    vmem = pl.BlockSpec(memory_space=pltpu.VMEM)
+    hbm = pl.BlockSpec(memory_space=pl.ANY)
     return pl.pallas_call(
-        gate_kernel,
+        functools.partial(exchange_kernel, dp_size, chips),
         out_shape=(
             jax.ShapeDtypeStruct((rows, width), jnp.float32),
-            jax.ShapeDtypeStruct((rows, width + router2.shape[1]), jnp.bfloat16),
+            jax.ShapeDtypeStruct((ex_size * rows, wide), jnp.bfloat16),
         ),
-        name="gate_rows",
-    )(attn_rows, rows_mine, gain.reshape(1, width), router2, chosen2)
+        in_specs=[vmem, hbm, vmem, vmem, vmem],
+        out_specs=(vmem, hbm),
+        scratch_shapes=[
+            pltpu.VMEM((rows, width), jnp.bfloat16),
+            pltpu.VMEM((dp_size - 1, rows, width), jnp.bfloat16),
+            pltpu.VMEM((rows, wide), jnp.bfloat16),
+            dma,
+            dma,
+            dma((dp_size - 1,)),
+            dma((dp_size - 1,)),
+        ]
+        + [dma((chips - 1,))] * 4
+        + [dma((2 * chips - 1,))] * 2,
+        compiler_params=pltpu.CompilerParams(
+            collective_id=0, has_side_effects=True, vmem_limit_bytes=40 << 20
+        ),
+        name="exchange",
+    )(projected, tokens, gain.reshape(1, width), router2, chosen2)
+
+
+def collect_kernel(
+    chips, part_ref, stream_ref, gain_ref, out_ref,
+    sib_ref, sum_ref, up_ref, dn_ref,
+    sib_send, sib_recv, up_send, up_recv, dn_send, dn_recv,
+):
+    rows = stream_ref.shape[0]
+    dp, ex = lax.axis_index("dp"), lax.axis_index("expert")
+    chip, core = ex // 2, ex % 2
+    upper, lower = chip < chips - 1, chip > 0
+    sibling = (dp, chip * 2 + 1 - core)
+    above = (dp, jnp.minimum(chip + 1, chips - 1) * 2 + core)
+    below = (dp, jnp.maximum(chip - 1, 0) * 2 + core)
+    greet([(chip >= 0, sibling), (upper, above), (lower, below)])
+    order = [k for pair in zip(range(chips), reversed(range(chips))) for k in pair][:chips]
+    swaps = []
+    for d in order:
+        copy = send(
+            part_ref.at[pl.ds((d * 2 + 1 - core) * rows, rows)],
+            sib_ref.at[d],
+            sib_send.at[d],
+            sib_recv.at[d],
+            sibling,
+        )
+        copy.start()
+        swaps.append(copy)
+    for d, copy in zip(order, swaps):
+        copy.wait_recv()
+        mine = part_ref[pl.ds((d * 2 + core) * rows, rows), :].astype(jnp.float32)
+        sum_ref[d] = (mine + sib_ref[d].astype(jnp.float32)).astype(jnp.bfloat16)
+
+    waits = []
+    for s in range(1, chips):
+        for index, (edge, target, buf, sends, recvs) in enumerate(
+            ((lower, below, dn_ref, dn_send, dn_recv), (upper, above, up_ref, up_send, up_recv))
+        ):
+            place = chips - 1 - chip if index == 0 else chip
+            hop = s - 1 - place
+            dest = hop if index == 0 else chips - 1 - hop
+            bounded = jnp.clip(dest, 0, chips - 1)
+            valid = edge & (hop >= 0) & ((dest < chip) if index == 0 else (dest > chip))
+            copy = send(
+                sum_ref.at[bounded], buf.at[s - 1], sends.at[s - 1], recvs.at[s - 1], target
+            )
+            if s > 1:
+
+                @pl.when(valid & (place > 0))
+                def _():
+                    total = sum_ref[bounded].astype(jnp.float32)
+                    total = total + buf[s - 2].astype(jnp.float32)
+                    sum_ref[bounded] = total.astype(jnp.bfloat16)
+
+            start_if(valid, copy)
+            waits.append((valid, copy))
+        for index, (edge, target, buf, sends, recvs) in enumerate(
+            ((upper, below, dn_ref, dn_send, dn_recv), (lower, above, up_ref, up_send, up_recv))
+        ):
+            place = chips - 1 - chip if index == 0 else chip
+            hop = s - place
+            dest = hop if index == 0 else chips - 1 - hop
+            valid = edge & (hop >= 0) & ((dest <= chip) if index == 0 else (dest >= chip))
+            copy = send(sum_ref.at[0], buf.at[s - 1], sends.at[s - 1], recvs.at[s - 1], target)
+            pl.when(valid)(copy.wait_recv)
+    last = chips - 2
+    total = stream_ref[...] + sum_ref[chip].astype(jnp.float32)
+    total = total + jnp.where(upper, dn_ref[last].astype(jnp.float32), 0.0)
+    total = total + jnp.where(lower, up_ref[last].astype(jnp.float32), 0.0)
+    out_ref[...] = rms_scale(total, gain_ref[...]).astype(jnp.bfloat16)
+    for cond, copy in waits:
+        pl.when(cond)(copy.wait_send)
+    for copy in swaps:
+        copy.wait_send()
+
+
+def collect(partial, stream, gain, ex_size):
+    rows, width = stream.shape
+    chips = ex_size // 2
+    dma = pltpu.SemaphoreType.DMA
+    vmem = pl.BlockSpec(memory_space=pltpu.VMEM)
+    blocks = pltpu.VMEM((chips, rows, width), jnp.bfloat16)
+    landing = pltpu.VMEM((chips - 1, rows, width), jnp.bfloat16)
+    return pl.pallas_call(
+        functools.partial(collect_kernel, chips),
+        out_shape=jax.ShapeDtypeStruct((rows, width), jnp.bfloat16),
+        in_specs=[vmem] * 3,
+        out_specs=vmem,
+        scratch_shapes=[blocks, blocks, landing, landing, dma((chips,)), dma((chips,))]
+        + [dma((chips - 1,))] * 4,
+        compiler_params=pltpu.CompilerParams(
+            collective_id=1, has_side_effects=True, vmem_limit_bytes=56 << 20
+        ),
+        name="collect",
+    )(partial, stream, gain.reshape(1, width))
 
 
 def experts_kernel(
@@ -314,16 +546,14 @@
     projected = attend(
         past_len, tokens, attn_gain, w_query, w_key, w_value, w_out, cache_keys, cache_values
     )
-    tok_dev = tokens.shape[0] // lax.axis_size("dp")
-    attn_rows = lax.psum_scatter(projected, "dp", scatter_dimension=0, tiled=True)
-    rows_mine = lax.dynamic_slice_in_dim(tokens, lax.axis_index("dp") * tok_dev, tok_dev, 0)
-    stream, extended = gate_rows(attn_rows, rows_mine, moe_gain, router2, chosen2)
-    gathered = lax.all_gather(extended, "expert", axis=0, tiled=True)
+    dp_size, ex_size = lax.axis_size("dp"), lax.axis_size("expert")
+    tok_dev = tokens.shape[0] // dp_size
+    stream, gathered = exchange(
+        projected, tokens, moe_gain, router2, chosen2, dp_size, ex_size
+    )
     me = lax.axis_index("expert").astype(jnp.int32).reshape(1)
     partial = run_experts(me, gathered, expert_in, expert_out, tok_dev)
-    mixed = lax.psum_scatter(partial, "expert", scatter_dimension=0, tiled=True)
-    combined = stream + mixed.astype(jnp.float32)
-    return rms_scale(combined, final_gain).astype(jnp.bfloat16)
+    return collect(partial, stream, final_gain, ex_size)
 
 
 def solution(mesh):

time: 217 us -> 184 us (0.85)
  waiting for transfers between devices: 114 us -> 0 us
  Pallas kernels: 73.1 us -> 169 us
  between operations: 13.2 us -> 0.12 us
  local copies, waits for them, and re-layouts: 8.42 us -> 11 us
  other arithmetic: 6.66 us -> 4.4 us
    pallas_call x1 -> x2, Pallas kernels: 2.6 us -> 102 us  [the longest x1 64.1 us: exchange(): pl.pallas_call(functools.partial(exchange_kernel, dp_size, chips), out_sh...]
    reduce_scatter x2 -> x0, waiting for transfers between devices: 73.6 us -> none  [the longest x1 41.6 us: shards(): mixed = lax.psum_scatter(partial, 'expert', scatter_dimension=0, tiled=True)]
    all_gather x1 -> x0, waiting for transfers between devices: 40.4 us -> none  [shards(): gathered = lax.all_gather(extended, 'expert', axis=0, tiled=True)]
    unnamed x24 -> x25, local copies, waits for them, and re-layouts: 5.21 us -> 9.6 us
    pallas_call x1, Pallas kernels: 40.2 us -> 36.9 us  [run_experts(): pl.pallas_call(functools.partial(experts_kernel, span), out_shape=jax.Sha...]
  transfers between devices with their start and end apart: 3 -> 0, of which waited for: 3 -> 0; matrix products, arithmetic and copies ran while one was open for 3% -> 0% of each run, Pallas kernels for 0% -> 0%
where the time goes in v3:
time: 184 us; the launch traced here: 185 us
  Pallas kernels  169 us (92%)
  local copies, waits for them, and re-layouts  11 us (6%)
  other arithmetic  4.4 us (2%)
    pallas_call x1, Pallas kernels, exchange(): pl.pallas_call(functools.partial(exchange_kernel, dp_size, chips), out_sh...  64.1 us
    pallas_call x1, Pallas kernels, collect(): pl.pallas_call(functools.partial(collect_kernel, chips), out_shape=jax.Sh...  37.9 us
    pallas_call x1, Pallas kernels, run_experts(): pl.pallas_call(functools.partial(experts_kernel, span), out_shape=jax.Sha...  36.9 us
    pallas_call x1, Pallas kernels, attend(): pl.pallas_call(functools.partial(attend_kernel, key_block), out_shape=jax...  30.1 us
    unnamed x25, local copies, waits for them, and re-layouts  9.6 us

profile of v3, /device:TPU:0, one launch (start us, length us, event | category | flops | bytes accessed | tf_op | source)
XLA Modules:
  0.0 184.9 jit_solution(11013246627464263546)
XLA Ops:
  0.0 0.0 copy-start
  0.0 0.9 convert_reduce_fusion
  0.9 3.3 %fusion.5 = pred[128,64]{0,1:T(8,128)(4,1)S(1)} fusion(s32[64]{0:T(128)S(1)} %compare_select_fusion, s32[128,8]{0,1:T(8,128)} %param.33, s32[64]{0:T(128)S(1)} %get-tuple-element.9, s32[128,8]{0,1:T(8,128)} %param.32, s32[64]{0:T(128)} %param.31, pred[64]{0:T(512)(128)(4,1)S(1)} %broadcast_compare_fusion), kind=kLoop, calls=%fused_computation.10 | loop fusion | flops 712704 | bytes 17216 | tf_op jit(solution)/shard_map/reduce_or | solution.py:519
  4.3 0.1 copy.22
  4.4 0.1 add_convert_fusion.chosen_ref
  4.5 0.7 reshape.30.gain_ref
  5.2 0.0 copy-start.3
  5.2 1.3 copy-done.3
  6.5 0.0 copy-start.4
  6.5 1.3 copy-done.4
  7.7 0.0 copy-start.6
  7.7 1.0 copy-done.6
  8.7 0.0 copy-start.7
  8.7 1.0 copy-done.7
  9.7 0.0 copy-start.8
  9.7 0.7 copy-done.8
  10.4 0.0 copy-start.11
  10.4 0.0 copy-start.9
  10.4 0.0 copy-start.1
  10.4 30.1 %attend.1.proj_ref = bf16[512,1536]{1,0:T(8,128)(2,1)S(1)} custom-call(s32[4]{0:T(128)S(1)} %copy-done.8, bf16[512,1536]{1,0:T(8,128)(2,1)} %tok_ref.3, f32[1,1536]{1,0:T(1,128)S(1)} %reshape.30.gain_ref, bf16[1536,384]{1,0:T(8,128)(2,1)S(1)} %copy-done.3, bf16[1536,128]{1,0:T(8,128)(2,1)S(1)} %copy-done.6, bf16[1536,128]{1,0:T(8,128)(2,1)S(1)} %copy-done.7, ...), custom_call_target="tpu_custom_call" | custom-call | tf_op jit(solution)/shard_map/attend/pallas_call | solution.py:123
  40.5 0.0 copy-done.11
  40.5 0.1 pad_add_fusion
  40.6 0.0 copy-done
  40.6 0.3 fusion.router_ref
  40.9 0.0 copy-done.9
  40.9 0.0 copy-done.1
  40.9 64.1 %exchange.1 = (f32[128,1536]{1,0:T(8,128)S(1)}, bf16[1024,1664]{1,0:T(8,128)(2,1)S(1)}) custom-call(bf16[512,1536]{1,0:T(8,128)(2,1)S(1)} %attend.1.proj_ref, bf16[512,1536]{1,0:T(8,128)(2,1)S(1)} %copy-done.1, f32[1,1536]{1,0:T(1,128)S(1)} %reshape.31.gain_ref, bf16[1536,128]{1,0:T(8,128)(2,1)S(1)} %fusion.router_ref, f32[128,128]{1,0:T(8,128)S(1)} %add_convert_fusion.chosen_ref), custom_call_target="tpu_custom_call" | custom-call | tf_op jit(solution)/shard_map/exchange/pallas_call | solution.py:286
  105.1 0.0 copy-start.2
  105.1 1.7 copy-done.2
  106.8 0.0 copy-start.5
  106.8 0.9 copy-done.5
  107.7 0.0 copy-start.10
  107.7 36.9 %run_experts.1.part_ref = bf16[1024,1536]{1,0:T(8,128)(2,1)} custom-call(s32[1]{0:T(128)} %bitcast.me_ref, bf16[1024,1664]{1,0:T(8,128)(2,1)} %copy-done.2, bf16[8,1536,1024]{2,1,0:T(8,128)(2,1)} %win_ref.1, bf16[8,512,1536]{2,1,0:T(8,128)(2,1)} %wout_ref.1), custom_call_target="tpu_custom_call" | custom-call | tf_op jit(solution)/shard_map/run_experts/pallas_call | solution.py:486
  144.6 0.0 copy-done.10
  144.6 0.6 reshape.32.gain_ref
  145.2 37.9 %collect.1 = bf16[128,1536]{1,0:T(8,128)(2,1)} custom-call(bf16[1024,1536]{1,0:T(8,128)(2,1)} %run_experts.1.part_ref, f32[128,1536]{1,0:T(8,128)} %copy-done.5, f32[1,1536]{1,0:T(1,128)} %reshape.32.gain_ref), custom_call_target="tpu_custom_call" | custom-call | tf_op jit(solution)/shard_map/collect/pallas_call | solution.py:392
  183.1 1.8 copy.26
  (3 shorter events, 0.0 us)
Async XLA Ops:
  0.0 40.6 %copy-start = (bf16[1536,40]{0,1:T(8,128)(2,1)S(1)}, bf16[1536,40]{0,1:T(8,128)(2,1)}, u32[]{:S(2)}) copy-start(bf16[1536,40]{0,1:T(8,128)(2,1)} %param.27) | copy-start | bytes 368644
  5.2 1.3 copy-start.3
  6.5 1.3 copy-start.4
  7.7 1.0 copy-start.6
  8.7 1.0 copy-start.7
  9.7 0.7 copy-start.8
  10.4 30.1 %copy-start.11 = (s32[64]{0:T(128)S(1)}, s32[64]{0:T(128)}, u32[]{:S(2)}) copy-start(s32[64]{0:T(128)} %param.31) | copy-start | bytes 772
  10.4 30.5 %copy-start.9 = (f32[1536]{0:T(1024)S(1)}, f32[1536]{0:T(1024)}, u32[]{:S(2)}) copy-start(f32[1536]{0:T(1024)} %param.26) | copy-start | bytes 18436
  10.4 30.5 %copy-start.1 = (bf16[512,1536]{1,0:T(8,128)(2,1)S(1)}, bf16[512,1536]{1,0:T(8,128)(2,1)}, u32[]{:S(2)}) copy-start(bf16[512,1536]{1,0:T(8,128)(2,1)} %tok_ref.3) | copy-start | bytes 4718596
  105.1 1.7 copy-start.2
  106.8 0.9 copy-start.5
  107.7 36.9 %copy-start.10 = (f32[1536]{0:T(1024)S(1)}, f32[1536]{0:T(1024)}, u32[]{:S(2)}) copy-start(f32[1536]{0:T(1024)} %param.30) | copy-start | bytes 18436

commit v4 on v3

--- a/solution.py
+++ b/solution.py
@@ -446,7 +446,7 @@
     rank_row = rank_t_ref[pl.ds(s, 1), :]
     count = jnp.max(rank_row).astype(jnp.int32) + 1
     chunk = math.gcd(rows, 512)
-    tile_rows = 256 if rows <= MOST_ROWS else 64
+    tile_rows = 320 if rows <= MOST_ROWS else 64
 
     def tile(index, carried):
         base = (index * tile_rows).astype(jnp.float32)

time: 184 us -> 192 us (1.043)
  Pallas kernels: 169 us -> 179 us
    pallas_call x1, Pallas kernels: 64.1 us -> 74.2 us  [exchange(): pl.pallas_call(functools.partial(exchange_kernel, dp_size, chips), out_sh...]
    pallas_call x1, Pallas kernels: 36.9 us -> 46.1 us  [run_experts(): pl.pallas_call(functools.partial(experts_kernel, span), out_shape=jax.Sha...]
    pallas_call x1, Pallas kernels: 30.1 us -> 22.2 us  [attend(): pl.pallas_call(functools.partial(attend_kernel, key_block), out_shape=jax...]
where the time goes in v4:
time: 192 us; the launch traced here: 195 us
  Pallas kernels  179 us (93%)
  local copies, waits for them, and re-layouts  11 us (6%)
  other arithmetic  4.4 us (2%)
    pallas_call x1, Pallas kernels, exchange(): pl.pallas_call(functools.partial(exchange_kernel, dp_size, chips), out_sh...  74.2 us
    pallas_call x1, Pallas kernels, run_experts(): pl.pallas_call(functools.partial(experts_kernel, span), out_shape=jax.Sha...  46.1 us
    pallas_call x1, Pallas kernels, collect(): pl.pallas_call(functools.partial(collect_kernel, chips), out_shape=jax.Sh...  36.3 us
    pallas_call x1, Pallas kernels, attend(): pl.pallas_call(functools.partial(attend_kernel, key_block), out_shape=jax...  22.2 us
    unnamed x25, local copies, waits for them, and re-layouts  9.6 us

profile of v4, /device:TPU:0, one launch (start us, length us, event | category | flops | bytes accessed | tf_op | source)
XLA Modules:
  0.0 194.6 jit_solution(17281881643438277294)
XLA Ops:
  0.0 0.0 copy-start
  0.0 0.9 convert_reduce_fusion
  0.9 3.3 %fusion.5 = pred[128,64]{0,1:T(8,128)(4,1)S(1)} fusion(s32[64]{0:T(128)S(1)} %compare_select_fusion, s32[128,8]{0,1:T(8,128)} %param.33, s32[64]{0:T(128)S(1)} %get-tuple-element.9, s32[128,8]{0,1:T(8,128)} %param.32, s32[64]{0:T(128)} %param.31, pred[64]{0:T(512)(128)(4,1)S(1)} %broadcast_compare_fusion), kind=kLoop, calls=%fused_computation.10 | loop fusion | flops 712704 | bytes 17216 | tf_op jit(solution)/shard_map/reduce_or | solution.py:519
  4.3 0.1 copy.22
  4.4 0.1 add_convert_fusion.chosen_ref
  4.5 0.7 reshape.30.gain_ref
  5.2 0.0 copy-start.3
  5.2 1.3 copy-done.3
  6.5 0.0 copy-start.4
  6.5 1.3 copy-done.4
  7.7 0.0 copy-start.6
  7.7 1.0 copy-done.6
  8.7 0.0 copy-start.7
  8.7 1.0 copy-done.7
  9.7 0.0 copy-start.8
  9.7 0.7 copy-done.8
  10.4 0.0 copy-start.11
  10.4 0.0 copy-start.9
  10.4 0.0 copy-start.1
  10.4 22.2 %attend.1.proj_ref = bf16[512,1536]{1,0:T(8,128)(2,1)S(1)} custom-call(s32[4]{0:T(128)S(1)} %copy-done.8, bf16[512,1536]{1,0:T(8,128)(2,1)} %tok_ref.3, f32[1,1536]{1,0:T(1,128)S(1)} %reshape.30.gain_ref, bf16[1536,384]{1,0:T(8,128)(2,1)S(1)} %copy-done.3, bf16[1536,128]{1,0:T(8,128)(2,1)S(1)} %copy-done.6, bf16[1536,128]{1,0:T(8,128)(2,1)S(1)} %copy-done.7, ...), custom_call_target="tpu_custom_call" | custom-call | tf_op jit(solution)/shard_map/attend/pallas_call | solution.py:123
  32.6 0.0 copy-done.11
  32.6 0.1 pad_add_fusion
  32.7 0.0 copy-done
  32.7 0.3 fusion.router_ref
  33.0 0.0 copy-done.9
  33.0 0.0 copy-done.1
  33.0 74.2 %exchange.1 = (f32[128,1536]{1,0:T(8,128)S(1)}, bf16[1024,1664]{1,0:T(8,128)(2,1)S(1)}) custom-call(bf16[512,1536]{1,0:T(8,128)(2,1)S(1)} %attend.1.proj_ref, bf16[512,1536]{1,0:T(8,128)(2,1)S(1)} %copy-done.1, f32[1,1536]{1,0:T(1,128)S(1)} %reshape.31.gain_ref, bf16[1536,128]{1,0:T(8,128)(2,1)S(1)} %fusion.router_ref, f32[128,128]{1,0:T(8,128)S(1)} %add_convert_fusion.chosen_ref), custom_call_target="tpu_custom_call" | custom-call | tf_op jit(solution)/shard_map/exchange/pallas_call | solution.py:286
  107.2 0.0 copy-start.2
  107.2 1.7 copy-done.2
  108.9 0.0 copy-start.5
  108.9 0.9 copy-done.5
  109.8 0.0 copy-start.10
  109.9 46.1 %run_experts.1.part_ref = bf16[1024,1536]{1,0:T(8,128)(2,1)} custom-call(s32[1]{0:T(128)} %bitcast.me_ref, bf16[1024,1664]{1,0:T(8,128)(2,1)} %copy-done.2, bf16[8,1536,1024]{2,1,0:T(8,128)(2,1)} %win_ref.1, bf16[8,512,1536]{2,1,0:T(8,128)(2,1)} %wout_ref.1), custom_call_target="tpu_custom_call" | custom-call | tf_op jit(solution)/shard_map/run_experts/pallas_call | solution.py:486
  156.0 0.0 copy-done.10
  156.0 0.6 reshape.32.gain_ref
  156.6 36.3 %collect.1 = bf16[128,1536]{1,0:T(8,128)(2,1)} custom-call(bf16[1024,1536]{1,0:T(8,128)(2,1)} %run_experts.1.part_ref, f32[128,1536]{1,0:T(8,128)} %copy-done.5, f32[1,1536]{1,0:T(1,128)} %reshape.32.gain_ref), custom_call_target="tpu_custom_call" | custom-call | tf_op jit(solution)/shard_map/collect/pallas_call | solution.py:392
  192.9 1.8 copy.26
  (3 shorter events, 0.0 us)
Async XLA Ops:
  0.0 32.7 %copy-start = (bf16[1536,40]{0,1:T(8,128)(2,1)S(1)}, bf16[1536,40]{0,1:T(8,128)(2,1)}, u32[]{:S(2)}) copy-start(bf16[1536,40]{0,1:T(8,128)(2,1)} %param.27) | copy-start | bytes 368644
  5.2 1.3 copy-start.3
  6.5 1.3 copy-start.4
  7.7 1.0 copy-start.6
  8.7 1.0 copy-start.7
  9.7 0.7 copy-start.8
  10.4 22.2 %copy-start.11 = (s32[64]{0:T(128)S(1)}, s32[64]{0:T(128)}, u32[]{:S(2)}) copy-start(s32[64]{0:T(128)} %param.31) | copy-start | bytes 772
  10.4 22.6 %copy-start.9 = (f32[1536]{0:T(1024)S(1)}, f32[1536]{0:T(1024)}, u32[]{:S(2)}) copy-start(f32[1536]{0:T(1024)} %param.26) | copy-start | bytes 18436
  10.4 22.7 %copy-start.1 = (bf16[512,1536]{1,0:T(8,128)(2,1)S(1)}, bf16[512,1536]{1,0:T(8,128)(2,1)}, u32[]{:S(2)}) copy-start(bf16[512,1536]{1,0:T(8,128)(2,1)} %tok_ref.3) | copy-start | bytes 4718596
  107.2 1.7 copy-start.2
  108.9 0.9 copy-start.5
  109.8 46.1 %copy-start.10 = (f32[1536]{0:T(1024)S(1)}, f32[1536]{0:T(1024)}, u32[]{:S(2)}) copy-start(f32[1536]{0:T(1024)} %param.30) | copy-start | bytes 18436
